TPU v7x, 256 devices: a whole 4x4x8 slice. The times are simulated.
256 devices in a mesh: tower: 2 (over y_lo), blk: 32 (over z, y_hi, core), mp: 4 (over x).
Axes of the slice: x: 4, y: 4 (y_hi: 2, y_lo: 2; y = y_hi * 2 + y_lo), z: 8, core: 2. Of those that a mesh axis runs over, the one named last changes fastest.
Arguments:
- image_feats: bfloat16 [32768, 5120], P('blk', 'mp'), may hold values from -6 to 6
- text_feats: bfloat16 [32768, 1280], P('blk', 'mp'), may hold values from -6 to 6
- image_proj: bfloat16 [5120, 1024], P('mp'), may hold values from -0.05729924 to 0.05729924
- text_proj: bfloat16 [1280, 1024], P('mp'), may hold values from -0.11459848 to 0.11459848
- logit_scale: float32 [], replicated, may hold values from 30 to 300
- pairs: int32 [32, 1024], P('blk'), may hold values from 0 to 1023, as said below
Outputs:
- image_loss: float32 [32768], P('blk')
- text_loss: float32 [32768], P('blk')
Inputs may be any that keep to these rules, and one draw needn't show every extreme that they name: Each row pairs[b] is a permutation of 0 to 1023: image b * 1024 + i is paired with caption b * 1024 + pairs[b, i].
All inputs are finite; a program needn't handle non-finite values.
Results may differ from a plain program's by a relative error of at most 0.0017.
Values may be sent and summed in bfloat16 or wider, within the bound.
A program may use at most 64 MiB of HBM per device.

v0:
```python
import jax
import jax.numpy as jnp
from jax import lax
from jax.sharding import PartitionSpec as P

WI = 5120
WT = 1280


def from_behind(value, axis, steps):
    count = lax.axis_size(axis)
    pairs = [(source, (source + steps) % count) for source in range(count)]
    return lax.ppermute(value, axis, pairs)


def combined_all(part, axis, combine):
    gathered = jax.tree.map(lambda a: lax.all_gather(a, axis), part)

    def take(source):
        return jax.tree.map(lambda a: lax.dynamic_index_in_dim(a, source, 0, False), gathered)

    return lax.fori_loop(
        1, lax.axis_size(axis), lambda source, state: combine(state, take(source)), take(0)
    )


def tile_stats(text_block, images, logit_scale):
    scores = logit_scale * lax.dot_general(
        text_block, images, (((1,), (1,)), ((), ())), preferred_element_type=jnp.float32
    )
    row_max = jnp.max(scores, axis=0)
    row_sum = jnp.sum(jnp.exp(scores - row_max[None, :]), axis=0)
    column_max = jnp.max(scores, axis=1)
    column_sum = jnp.sum(jnp.exp(scores - column_max[:, None]), axis=1)
    return (scores, row_max, row_sum, column_max, column_sum)


def add_rows(old_max, old_sum, tile_max, tile_sum):
    new_max = jnp.maximum(old_max, tile_max)
    return (new_max, old_sum * jnp.exp(old_max - new_max) + tile_sum * jnp.exp(tile_max - new_max))


def combine_rows(first, second):
    merged_max, merged_sum = add_rows(first[0], first[1], second[0], second[1])
    return (merged_max, merged_sum, first[2] + second[2])


def local_sums(operand):
    values = operand.astype(jnp.float32)
    return (jnp.sum(values, axis=1), jnp.sum(values * values, axis=1))


def on_device(image_feats, text_feats, image_proj, text_proj, logit_scale, pairs):
    tower_index = lax.axis_index("tower")
    is_image = tower_index == 0
    mp_count = lax.axis_size("mp")
    mp_index = lax.axis_index("mp")
    blk_count = lax.axis_size("blk")
    blk_index = lax.axis_index("blk")
    row_total = image_feats.shape[0]
    piece = row_total // (2 * mp_count)
    first_sum, second_sum = lax.cond(
        is_image, lambda: local_sums(image_feats), lambda: local_sums(text_feats)
    )
    first_sum, second_sum = lax.psum((first_sum, second_sum), "mp")
    feature_width = jnp.where(is_image, jnp.float32(WI), jnp.float32(WT))
    row_mean = first_sum / feature_width
    inverse = lax.rsqrt(second_sum / feature_width - row_mean * row_mean + 1e-06)

    def project_rows(features, weights):
        values = features.astype(jnp.float32)
        normed = ((values - row_mean[:, None]) * inverse[:, None]).astype(jnp.bfloat16)
        return jnp.dot(normed, weights, preferred_element_type=jnp.float32)

    projected = lax.psum_scatter(
        lax.cond(
            is_image,
            lambda: project_rows(image_feats, image_proj),
            lambda: project_rows(text_feats, text_proj),
        ),
        "mp",
        scatter_dimension=0,
        tiled=True,
    )
    length = lax.rsqrt(jnp.sum(projected * projected, axis=1, keepdims=True) + 1e-06)
    embedded = (projected * length).astype(jnp.bfloat16)
    joined = lax.all_gather(embedded, ("tower", "mp"), axis=0, tiled=True)
    images = joined[:row_total]
    piece_index = tower_index * mp_count + mp_index
    captions = lax.dynamic_slice_in_dim(joined, row_total + piece_index * piece, piece, 0)
    own_pairs = pairs[0]
    scores, row_max, row_sum, column_max, column_sum = tile_stats(captions, images, logit_scale)
    matches = own_pairs[None, :] == piece_index * piece + lax.broadcasted_iota(
        jnp.int32, (piece, 1), 0
    )
    picked = jnp.where(matches, scores, 0.0)
    image_positive = jnp.sum(picked, axis=0)
    caption_positive = jnp.sum(picked, axis=1)
    slot_max = jnp.zeros((blk_count, piece), jnp.float32)
    slot_sum = jnp.zeros((blk_count, piece), jnp.float32)
    slot_max = lax.dynamic_update_slice(slot_max, column_max[None, :], (blk_index, 0))
    slot_sum = lax.dynamic_update_slice(slot_sum, column_sum[None, :], (blk_index, 0))

    def advance(visit_step, state):
        text_block, running_max, running_sum, stored_max, stored_sum = state
        text_block = from_behind(text_block, "blk", 1)
        unused, tile_max, tile_sum, block_max, block_sum = tile_stats(
            text_block, images, logit_scale
        )
        running_max, running_sum = add_rows(running_max, running_sum, tile_max, tile_sum)
        source = (blk_index - visit_step) % blk_count
        stored_max = lax.dynamic_update_slice(stored_max, block_max[None, :], (source, 0))
        stored_sum = lax.dynamic_update_slice(stored_sum, block_sum[None, :], (source, 0))
        return (text_block, running_max, running_sum, stored_max, stored_sum)

    final_state = lax.fori_loop(
        1, blk_count, advance, (captions, row_max, row_sum, slot_max, slot_sum)
    )
    row_max, row_sum, slot_max, slot_sum = (
        final_state[1],
        final_state[2],
        final_state[3],
        final_state[4],
    )
    slot_max, slot_sum = (
        lax.all_to_all(slot_max, "blk", split_axis=0, concat_axis=0, tiled=True),
        lax.all_to_all(slot_sum, "blk", split_axis=0, concat_axis=0, tiled=True),
    )
    whole_max = jnp.max(slot_max, axis=0)
    caption_lse = whole_max + jnp.log(
        jnp.sum(slot_sum * jnp.exp(slot_max - whole_max[None, :]), axis=0)
    )
    caption_loss = caption_lse - caption_positive
    merged_max, merged_sum, merged_positive = combined_all(
        (row_max, row_sum, image_positive), ("tower", "mp"), combine_rows
    )
    image_loss = merged_max + jnp.log(merged_sum) - merged_positive
    all_losses = lax.all_gather(caption_loss, ("tower", "mp"), axis=0, tiled=True)
    return (image_loss, all_losses)


def solution(mesh):
    return jax.shard_map(
        on_device,
        mesh=mesh,
        in_specs=(
            P("blk", "mp"),
            P("blk", "mp"),
            P("mp", None),
            P("mp", None),
            P(),
            P("blk", None),
        ),
        out_specs=(P("blk"), P("blk")),
        check_vma=False,
    )
```

profile of v0, /device:TPU:8, one launch (start us, length us, event | category | flops | bytes accessed | tf_op | source)
XLA Modules:
  0.0 714.1 jit_solution(11879845343532670806)
XLA Ops:
  9.1 10.6 %all-reduce = (f32[1024]{0:T(1024)S(1)}, f32[1024]{0:T(1024)S(1)}) all-reduce(f32[1024]{0:T(1024)S(1)} %get-tuple-element.435, f32[1024]{0:T(1024)S(1)} %get-tuple-element.436), channel_id=1, replica_groups=mesh['tower'=2,'blk'=32,'mp'=4] {'mp'}, use_global_device_ids=true, to_apply=%region_6.0 | all-reduce | flops 2048 | bytes 16384 | tf_op jit(solution)/shard_map/psum | solution.py:65
  24.5 53.6 %reduce-scatter.2.cloned.1.call-done = f32[256,1024]{1,0:T(8,128)} async-done(((f32[1024,1024]{1,0:T(8,128)}), f32[256,1024]{1,0:T(8,128)}) %reduce-scatter.2.cloned.1.call-update) | async-done | bytes 1048592 | tf_op jit(solution)/shard_map/reduce_scatter | solution.py:75
  82.4 53.4 %all-gather.6.cloned.1.call-done = bf16[2048,1024]{1,0:T(8,128)(2,1)} async-done(((bf16[256,1024]{1,0:T(8,128)(2,1)}), bf16[2048,1024]{1,0:T(8,128)(2,1)}) %all-gather.6.cloned.1.call-update) | async-done | bytes 4194320 | tf_op jit(solution)/shard_map/all_gather | solution.py:87
  143.4 431.3 %while.42 = (s32[]{:T(128)}, bf16[128,1024]{1,0:T(8,128)(2,1)S(1)}, f32[1024]{0:T(1024)S(1)}, f32[1024]{0:T(1024)S(1)}, f32[32,128]{1,0:T(8,128)}, /*index=5*/f3...) while((s32[]{:T(128)}, bf16[128,1024]{1,0:T(8,128)(2,1)S(1)}, ...), condition=%wide.region_21.22_spmd, body=%wide.region_16.21_spmd.sunk | while | flops 269356800 | bytes 5021516 | solution.py:116
  143.4 9.4 %collective-permute-done = bf16[128,1024]{1,0:T(8,128)(2,1)S(1)} collective-permute-done((bf16[128,1024]{1,0:T(8,128)(2,1)S(1)}, bf16[128,1024]{1,0:T(8,128)(2,1)S(1)}, u32[]{:S(2)}, u32[]{:S(2)}) %collective-permute-start) | collective-permute-done | bytes 262176 | tf_op jit(solution)/shard_map/while/body/eval_jaxpr/ppermute | solution.py:13
  157.3 9.4 %collective-permute-done = bf16[128,1024]{1,0:T(8,128)(2,1)S(1)} collective-permute-done((bf16[128,1024]{1,0:T(8,128)(2,1)S(1)}, bf16[128,1024]{1,0:T(8,128)(2,1)S(1)}, u32[]{:S(2)}, u32[]{:S(2)}) %collective-permute-start) | collective-permute-done | bytes 262176 | tf_op jit(solution)/shard_map/while/body/eval_jaxpr/ppermute | solution.py:13
  171.2 9.4 %collective-permute-done = bf16[128,1024]{1,0:T(8,128)(2,1)S(1)} collective-permute-done((bf16[128,1024]{1,0:T(8,128)(2,1)S(1)}, bf16[128,1024]{1,0:T(8,128)(2,1)S(1)}, u32[]{:S(2)}, u32[]{:S(2)}) %collective-permute-start) | collective-permute-done | bytes 262176 | tf_op jit(solution)/shard_map/while/body/eval_jaxpr/ppermute | solution.py:13
  185.2 9.4 %collective-permute-done = bf16[128,1024]{1,0:T(8,128)(2,1)S(1)} collective-permute-done((bf16[128,1024]{1,0:T(8,128)(2,1)S(1)}, bf16[128,1024]{1,0:T(8,128)(2,1)S(1)}, u32[]{:S(2)}, u32[]{:S(2)}) %collective-permute-start) | collective-permute-done | bytes 262176 | tf_op jit(solution)/shard_map/while/body/eval_jaxpr/ppermute | solution.py:13
  199.1 9.4 %collective-permute-done = bf16[128,1024]{1,0:T(8,128)(2,1)S(1)} collective-permute-done((bf16[128,1024]{1,0:T(8,128)(2,1)S(1)}, bf16[128,1024]{1,0:T(8,128)(2,1)S(1)}, u32[]{:S(2)}, u32[]{:S(2)}) %collective-permute-start) | collective-permute-done | bytes 262176 | tf_op jit(solution)/shard_map/while/body/eval_jaxpr/ppermute | solution.py:13
  213.0 9.4 %collective-permute-done = bf16[128,1024]{1,0:T(8,128)(2,1)S(1)} collective-permute-done((bf16[128,1024]{1,0:T(8,128)(2,1)S(1)}, bf16[128,1024]{1,0:T(8,128)(2,1)S(1)}, u32[]{:S(2)}, u32[]{:S(2)}) %collective-permute-start) | collective-permute-done | bytes 262176 | tf_op jit(solution)/shard_map/while/body/eval_jaxpr/ppermute | solution.py:13
  226.9 9.4 %collective-permute-done = bf16[128,1024]{1,0:T(8,128)(2,1)S(1)} collective-permute-done((bf16[128,1024]{1,0:T(8,128)(2,1)S(1)}, bf16[128,1024]{1,0:T(8,128)(2,1)S(1)}, u32[]{:S(2)}, u32[]{:S(2)}) %collective-permute-start) | collective-permute-done | bytes 262176 | tf_op jit(solution)/shard_map/while/body/eval_jaxpr/ppermute | solution.py:13
  268.6 9.4 %collective-permute-done = bf16[128,1024]{1,0:T(8,128)(2,1)S(1)} collective-permute-done((bf16[128,1024]{1,0:T(8,128)(2,1)S(1)}, bf16[128,1024]{1,0:T(8,128)(2,1)S(1)}, u32[]{:S(2)}, u32[]{:S(2)}) %collective-permute-start) | collective-permute-done | bytes 262176 | tf_op jit(solution)/shard_map/while/body/eval_jaxpr/ppermute | solution.py:13
  282.5 9.4 %collective-permute-done = bf16[128,1024]{1,0:T(8,128)(2,1)S(1)} collective-permute-done((bf16[128,1024]{1,0:T(8,128)(2,1)S(1)}, bf16[128,1024]{1,0:T(8,128)(2,1)S(1)}, u32[]{:S(2)}, u32[]{:S(2)}) %collective-permute-start) | collective-permute-done | bytes 262176 | tf_op jit(solution)/shard_map/while/body/eval_jaxpr/ppermute | solution.py:13
  296.5 9.4 %collective-permute-done = bf16[128,1024]{1,0:T(8,128)(2,1)S(1)} collective-permute-done((bf16[128,1024]{1,0:T(8,128)(2,1)S(1)}, bf16[128,1024]{1,0:T(8,128)(2,1)S(1)}, u32[]{:S(2)}, u32[]{:S(2)}) %collective-permute-start) | collective-permute-done | bytes 262176 | tf_op jit(solution)/shard_map/while/body/eval_jaxpr/ppermute | solution.py:13
  310.4 9.4 %collective-permute-done = bf16[128,1024]{1,0:T(8,128)(2,1)S(1)} collective-permute-done((bf16[128,1024]{1,0:T(8,128)(2,1)S(1)}, bf16[128,1024]{1,0:T(8,128)(2,1)S(1)}, u32[]{:S(2)}, u32[]{:S(2)}) %collective-permute-start) | collective-permute-done | bytes 262176 | tf_op jit(solution)/shard_map/while/body/eval_jaxpr/ppermute | solution.py:13
  324.3 9.4 %collective-permute-done = bf16[128,1024]{1,0:T(8,128)(2,1)S(1)} collective-permute-done((bf16[128,1024]{1,0:T(8,128)(2,1)S(1)}, bf16[128,1024]{1,0:T(8,128)(2,1)S(1)}, u32[]{:S(2)}, u32[]{:S(2)}) %collective-permute-start) | collective-permute-done | bytes 262176 | tf_op jit(solution)/shard_map/while/body/eval_jaxpr/ppermute | solution.py:13
  366.0 9.4 %collective-permute-done = bf16[128,1024]{1,0:T(8,128)(2,1)S(1)} collective-permute-done((bf16[128,1024]{1,0:T(8,128)(2,1)S(1)}, bf16[128,1024]{1,0:T(8,128)(2,1)S(1)}, u32[]{:S(2)}, u32[]{:S(2)}) %collective-permute-start) | collective-permute-done | bytes 262176 | tf_op jit(solution)/shard_map/while/body/eval_jaxpr/ppermute | solution.py:13
  379.9 9.4 %collective-permute-done = bf16[128,1024]{1,0:T(8,128)(2,1)S(1)} collective-permute-done((bf16[128,1024]{1,0:T(8,128)(2,1)S(1)}, bf16[128,1024]{1,0:T(8,128)(2,1)S(1)}, u32[]{:S(2)}, u32[]{:S(2)}) %collective-permute-start) | collective-permute-done | bytes 262176 | tf_op jit(solution)/shard_map/while/body/eval_jaxpr/ppermute | solution.py:13
  393.8 9.4 %collective-permute-done = bf16[128,1024]{1,0:T(8,128)(2,1)S(1)} collective-permute-done((bf16[128,1024]{1,0:T(8,128)(2,1)S(1)}, bf16[128,1024]{1,0:T(8,128)(2,1)S(1)}, u32[]{:S(2)}, u32[]{:S(2)}) %collective-permute-start) | collective-permute-done | bytes 262176 | tf_op jit(solution)/shard_map/while/body/eval_jaxpr/ppermute | solution.py:13
  407.7 9.4 %collective-permute-done = bf16[128,1024]{1,0:T(8,128)(2,1)S(1)} collective-permute-done((bf16[128,1024]{1,0:T(8,128)(2,1)S(1)}, bf16[128,1024]{1,0:T(8,128)(2,1)S(1)}, u32[]{:S(2)}, u32[]{:S(2)}) %collective-permute-start) | collective-permute-done | bytes 262176 | tf_op jit(solution)/shard_map/while/body/eval_jaxpr/ppermute | solution.py:13
  421.7 9.4 %collective-permute-done = bf16[128,1024]{1,0:T(8,128)(2,1)S(1)} collective-permute-done((bf16[128,1024]{1,0:T(8,128)(2,1)S(1)}, bf16[128,1024]{1,0:T(8,128)(2,1)S(1)}, u32[]{:S(2)}, u32[]{:S(2)}) %collective-permute-start) | collective-permute-done | bytes 262176 | tf_op jit(solution)/shard_map/while/body/eval_jaxpr/ppermute | solution.py:13
  435.6 9.4 %collective-permute-done = bf16[128,1024]{1,0:T(8,128)(2,1)S(1)} collective-permute-done((bf16[128,1024]{1,0:T(8,128)(2,1)S(1)}, bf16[128,1024]{1,0:T(8,128)(2,1)S(1)}, u32[]{:S(2)}, u32[]{:S(2)}) %collective-permute-start) | collective-permute-done | bytes 262176 | tf_op jit(solution)/shard_map/while/body/eval_jaxpr/ppermute | solution.py:13
  449.5 9.4 %collective-permute-done = bf16[128,1024]{1,0:T(8,128)(2,1)S(1)} collective-permute-done((bf16[128,1024]{1,0:T(8,128)(2,1)S(1)}, bf16[128,1024]{1,0:T(8,128)(2,1)S(1)}, u32[]{:S(2)}, u32[]{:S(2)}) %collective-permute-start) | collective-permute-done | bytes 262176 | tf_op jit(solution)/shard_map/while/body/eval_jaxpr/ppermute | solution.py:13
  463.4 9.4 %collective-permute-done = bf16[128,1024]{1,0:T(8,128)(2,1)S(1)} collective-permute-done((bf16[128,1024]{1,0:T(8,128)(2,1)S(1)}, bf16[128,1024]{1,0:T(8,128)(2,1)S(1)}, u32[]{:S(2)}, u32[]{:S(2)}) %collective-permute-start) | collective-permute-done | bytes 262176 | tf_op jit(solution)/shard_map/while/body/eval_jaxpr/ppermute | solution.py:13
  477.3 9.4 %collective-permute-done = bf16[128,1024]{1,0:T(8,128)(2,1)S(1)} collective-permute-done((bf16[128,1024]{1,0:T(8,128)(2,1)S(1)}, bf16[128,1024]{1,0:T(8,128)(2,1)S(1)}, u32[]{:S(2)}, u32[]{:S(2)}) %collective-permute-start) | collective-permute-done | bytes 262176 | tf_op jit(solution)/shard_map/while/body/eval_jaxpr/ppermute | solution.py:13
  491.2 9.4 %collective-permute-done = bf16[128,1024]{1,0:T(8,128)(2,1)S(1)} collective-permute-done((bf16[128,1024]{1,0:T(8,128)(2,1)S(1)}, bf16[128,1024]{1,0:T(8,128)(2,1)S(1)}, u32[]{:S(2)}, u32[]{:S(2)}) %collective-permute-start) | collective-permute-done | bytes 262176 | tf_op jit(solution)/shard_map/while/body/eval_jaxpr/ppermute | solution.py:13
  505.1 9.4 %collective-permute-done = bf16[128,1024]{1,0:T(8,128)(2,1)S(1)} collective-permute-done((bf16[128,1024]{1,0:T(8,128)(2,1)S(1)}, bf16[128,1024]{1,0:T(8,128)(2,1)S(1)}, u32[]{:S(2)}, u32[]{:S(2)}) %collective-permute-start) | collective-permute-done | bytes 262176 | tf_op jit(solution)/shard_map/while/body/eval_jaxpr/ppermute | solution.py:13
  560.8 9.4 %collective-permute-done = bf16[128,1024]{1,0:T(8,128)(2,1)S(1)} collective-permute-done((bf16[128,1024]{1,0:T(8,128)(2,1)S(1)}, bf16[128,1024]{1,0:T(8,128)(2,1)S(1)}, u32[]{:S(2)}, u32[]{:S(2)}) %collective-permute-start) | collective-permute-done | bytes 262176 | tf_op jit(solution)/shard_map/while/body/eval_jaxpr/ppermute | solution.py:13
  574.7 28.3 %all-gather = f32[8192]{0:T(1024)S(1)} all-gather(f32[1024]{0:T(1024)S(1)} %get-tuple-element.437), channel_id=2, replica_groups=mesh['tower'=2,'blk'=32,'mp'=4] {'tower','mp'}, dimensions={0}, use_global_device_ids=true | all-gather | bytes 36864 | tf_op jit(solution)/shard_map/all_gather | solution.py:17
  603.0 28.3 %all-gather.1 = f32[8192]{0:T(1024)S(1)} all-gather(f32[1024]{0:T(1024)S(1)} %get-tuple-element.438), channel_id=3, replica_groups=mesh['tower'=2,'blk'=32,'mp'=4] {'tower','mp'}, dimensions={0}, use_global_device_ids=true | all-gather | bytes 36864 | tf_op jit(solution)/shard_map/all_gather | solution.py:17
  631.2 28.3 %all-gather.2 = f32[8192]{0:T(1024)S(1)} all-gather(f32[1024]{0:T(1024)S(1)} %get-tuple-element.466), channel_id=4, replica_groups=mesh['tower'=2,'blk'=32,'mp'=4] {'tower','mp'}, dimensions={0}, use_global_device_ids=true | all-gather | bytes 36864 | tf_op jit(solution)/shard_map/all_gather | solution.py:17
  690.2 16.5 %all-gather.3 = f32[8,1,128]{2,1,0:T(1,128)S(1)} all-gather(f32[1,1,128]{2,1,0:T(1,128)S(1)} %subtract_bitcast_fusion), channel_id=1, replica_groups=mesh['tower'=2,'blk'=32,'mp'=4] {'tower','mp'}, dimensions={0}, use_global_device_ids=true | all-gather | bytes 4608 | tf_op jit(solution)/shard_map/all_gather | solution.py:138
  (296 shorter events, 260.5 us)
Async XLA Ops:
  7.2 71.0 %reduce-scatter.2.cloned.1.call-start = ((), (), s32[]{:S(2)}) async-start(), calls=%async_computation.3 | async-start | bytes 5242880 | tf_op jit(solution)/shard_map/reduce_scatter | solution.py:75
  24.5 111.3 %all-gather.6.cloned.1.call-start = ((), (), s32[]{:S(2)}) async-start(), calls=%async_computation.4 | async-start | bytes 4718592 | tf_op jit(solution)/shard_map/all_gather | solution.py:87
  157.2 9.5 %collective-permute-start = (bf16[128,1024]{1,0:T(8,128)(2,1)S(1)}, bf16[128,1024]{1,0:T(8,128)(2,1)S(1)}, u32[]{:S(2)}, u32[]{:S(2)}) collective-permute-start(bf16[128,1024]{1,0:T(8,128)(2,1)S(1)} %get-tuple-element.653), channel_id=1, source_target_pairs={{0,4},{4,8},{8,12},{12,16},{16,20},{20,24},{24,28},{28,32},{32,36}... | collective-permute-start | bytes 786440 | tf_op jit(solution)/shard_map/while/body/eval_jaxpr/ppermute | solution.py:13
  171.1 9.5 %collective-permute-start = (bf16[128,1024]{1,0:T(8,128)(2,1)S(1)}, bf16[128,1024]{1,0:T(8,128)(2,1)S(1)}, u32[]{:S(2)}, u32[]{:S(2)}) collective-permute-start(bf16[128,1024]{1,0:T(8,128)(2,1)S(1)} %get-tuple-element.653), channel_id=1, source_target_pairs={{0,4},{4,8},{8,12},{12,16},{16,20},{20,24},{24,28},{28,32},{32,36}... | collective-permute-start | bytes 786440 | tf_op jit(solution)/shard_map/while/body/eval_jaxpr/ppermute | solution.py:13
  185.0 9.5 %collective-permute-start = (bf16[128,1024]{1,0:T(8,128)(2,1)S(1)}, bf16[128,1024]{1,0:T(8,128)(2,1)S(1)}, u32[]{:S(2)}, u32[]{:S(2)}) collective-permute-start(bf16[128,1024]{1,0:T(8,128)(2,1)S(1)} %get-tuple-element.653), channel_id=1, source_target_pairs={{0,4},{4,8},{8,12},{12,16},{16,20},{20,24},{24,28},{28,32},{32,36}... | collective-permute-start | bytes 786440 | tf_op jit(solution)/shard_map/while/body/eval_jaxpr/ppermute | solution.py:13
  199.0 9.5 %collective-permute-start = (bf16[128,1024]{1,0:T(8,128)(2,1)S(1)}, bf16[128,1024]{1,0:T(8,128)(2,1)S(1)}, u32[]{:S(2)}, u32[]{:S(2)}) collective-permute-start(bf16[128,1024]{1,0:T(8,128)(2,1)S(1)} %get-tuple-element.653), channel_id=1, source_target_pairs={{0,4},{4,8},{8,12},{12,16},{16,20},{20,24},{24,28},{28,32},{32,36}... | collective-permute-start | bytes 786440 | tf_op jit(solution)/shard_map/while/body/eval_jaxpr/ppermute | solution.py:13
  212.9 9.5 %collective-permute-start = (bf16[128,1024]{1,0:T(8,128)(2,1)S(1)}, bf16[128,1024]{1,0:T(8,128)(2,1)S(1)}, u32[]{:S(2)}, u32[]{:S(2)}) collective-permute-start(bf16[128,1024]{1,0:T(8,128)(2,1)S(1)} %get-tuple-element.653), channel_id=1, source_target_pairs={{0,4},{4,8},{8,12},{12,16},{16,20},{20,24},{24,28},{28,32},{32,36}... | collective-permute-start | bytes 786440 | tf_op jit(solution)/shard_map/while/body/eval_jaxpr/ppermute | solution.py:13
  226.8 9.5 %collective-permute-start = (bf16[128,1024]{1,0:T(8,128)(2,1)S(1)}, bf16[128,1024]{1,0:T(8,128)(2,1)S(1)}, u32[]{:S(2)}, u32[]{:S(2)}) collective-permute-start(bf16[128,1024]{1,0:T(8,128)(2,1)S(1)} %get-tuple-element.653), channel_id=1, source_target_pairs={{0,4},{4,8},{8,12},{12,16},{16,20},{20,24},{24,28},{28,32},{32,36}... | collective-permute-start | bytes 786440 | tf_op jit(solution)/shard_map/while/body/eval_jaxpr/ppermute | solution.py:13
  240.7 9.5 %collective-permute-start = (bf16[128,1024]{1,0:T(8,128)(2,1)S(1)}, bf16[128,1024]{1,0:T(8,128)(2,1)S(1)}, u32[]{:S(2)}, u32[]{:S(2)}) collective-permute-start(bf16[128,1024]{1,0:T(8,128)(2,1)S(1)} %get-tuple-element.653), channel_id=1, source_target_pairs={{0,4},{4,8},{8,12},{12,16},{16,20},{20,24},{24,28},{28,32},{32,36}... | collective-permute-start | bytes 786440 | tf_op jit(solution)/shard_map/while/body/eval_jaxpr/ppermute | solution.py:13
  254.6 9.5 %collective-permute-start = (bf16[128,1024]{1,0:T(8,128)(2,1)S(1)}, bf16[128,1024]{1,0:T(8,128)(2,1)S(1)}, u32[]{:S(2)}, u32[]{:S(2)}) collective-permute-start(bf16[128,1024]{1,0:T(8,128)(2,1)S(1)} %get-tuple-element.653), channel_id=1, source_target_pairs={{0,4},{4,8},{8,12},{12,16},{16,20},{20,24},{24,28},{28,32},{32,36}... | collective-permute-start | bytes 786440 | tf_op jit(solution)/shard_map/while/body/eval_jaxpr/ppermute | solution.py:13
  268.5 9.5 %collective-permute-start = (bf16[128,1024]{1,0:T(8,128)(2,1)S(1)}, bf16[128,1024]{1,0:T(8,128)(2,1)S(1)}, u32[]{:S(2)}, u32[]{:S(2)}) collective-permute-start(bf16[128,1024]{1,0:T(8,128)(2,1)S(1)} %get-tuple-element.653), channel_id=1, source_target_pairs={{0,4},{4,8},{8,12},{12,16},{16,20},{20,24},{24,28},{28,32},{32,36}... | collective-permute-start | bytes 786440 | tf_op jit(solution)/shard_map/while/body/eval_jaxpr/ppermute | solution.py:13
  282.4 9.5 %collective-permute-start = (bf16[128,1024]{1,0:T(8,128)(2,1)S(1)}, bf16[128,1024]{1,0:T(8,128)(2,1)S(1)}, u32[]{:S(2)}, u32[]{:S(2)}) collective-permute-start(bf16[128,1024]{1,0:T(8,128)(2,1)S(1)} %get-tuple-element.653), channel_id=1, source_target_pairs={{0,4},{4,8},{8,12},{12,16},{16,20},{20,24},{24,28},{28,32},{32,36}... | collective-permute-start | bytes 786440 | tf_op jit(solution)/shard_map/while/body/eval_jaxpr/ppermute | solution.py:13
  296.3 9.5 %collective-permute-start = (bf16[128,1024]{1,0:T(8,128)(2,1)S(1)}, bf16[128,1024]{1,0:T(8,128)(2,1)S(1)}, u32[]{:S(2)}, u32[]{:S(2)}) collective-permute-start(bf16[128,1024]{1,0:T(8,128)(2,1)S(1)} %get-tuple-element.653), channel_id=1, source_target_pairs={{0,4},{4,8},{8,12},{12,16},{16,20},{20,24},{24,28},{28,32},{32,36}... | collective-permute-start | bytes 786440 | tf_op jit(solution)/shard_map/while/body/eval_jaxpr/ppermute | solution.py:13
  310.2 9.5 %collective-permute-start = (bf16[128,1024]{1,0:T(8,128)(2,1)S(1)}, bf16[128,1024]{1,0:T(8,128)(2,1)S(1)}, u32[]{:S(2)}, u32[]{:S(2)}) collective-permute-start(bf16[128,1024]{1,0:T(8,128)(2,1)S(1)} %get-tuple-element.653), channel_id=1, source_target_pairs={{0,4},{4,8},{8,12},{12,16},{16,20},{20,24},{24,28},{28,32},{32,36}... | collective-permute-start | bytes 786440 | tf_op jit(solution)/shard_map/while/body/eval_jaxpr/ppermute | solution.py:13
  324.2 9.5 %collective-permute-start = (bf16[128,1024]{1,0:T(8,128)(2,1)S(1)}, bf16[128,1024]{1,0:T(8,128)(2,1)S(1)}, u32[]{:S(2)}, u32[]{:S(2)}) collective-permute-start(bf16[128,1024]{1,0:T(8,128)(2,1)S(1)} %get-tuple-element.653), channel_id=1, source_target_pairs={{0,4},{4,8},{8,12},{12,16},{16,20},{20,24},{24,28},{28,32},{32,36}... | collective-permute-start | bytes 786440 | tf_op jit(solution)/shard_map/while/body/eval_jaxpr/ppermute | solution.py:13
  338.1 9.5 %collective-permute-start = (bf16[128,1024]{1,0:T(8,128)(2,1)S(1)}, bf16[128,1024]{1,0:T(8,128)(2,1)S(1)}, u32[]{:S(2)}, u32[]{:S(2)}) collective-permute-start(bf16[128,1024]{1,0:T(8,128)(2,1)S(1)} %get-tuple-element.653), channel_id=1, source_target_pairs={{0,4},{4,8},{8,12},{12,16},{16,20},{20,24},{24,28},{28,32},{32,36}... | collective-permute-start | bytes 786440 | tf_op jit(solution)/shard_map/while/body/eval_jaxpr/ppermute | solution.py:13
  352.0 9.5 %collective-permute-start = (bf16[128,1024]{1,0:T(8,128)(2,1)S(1)}, bf16[128,1024]{1,0:T(8,128)(2,1)S(1)}, u32[]{:S(2)}, u32[]{:S(2)}) collective-permute-start(bf16[128,1024]{1,0:T(8,128)(2,1)S(1)} %get-tuple-element.653), channel_id=1, source_target_pairs={{0,4},{4,8},{8,12},{12,16},{16,20},{20,24},{24,28},{28,32},{32,36}... | collective-permute-start | bytes 786440 | tf_op jit(solution)/shard_map/while/body/eval_jaxpr/ppermute | solution.py:13
  365.9 9.5 %collective-permute-start = (bf16[128,1024]{1,0:T(8,128)(2,1)S(1)}, bf16[128,1024]{1,0:T(8,128)(2,1)S(1)}, u32[]{:S(2)}, u32[]{:S(2)}) collective-permute-start(bf16[128,1024]{1,0:T(8,128)(2,1)S(1)} %get-tuple-element.653), channel_id=1, source_target_pairs={{0,4},{4,8},{8,12},{12,16},{16,20},{20,24},{24,28},{28,32},{32,36}... | collective-permute-start | bytes 786440 | tf_op jit(solution)/shard_map/while/body/eval_jaxpr/ppermute | solution.py:13
  379.8 9.5 %collective-permute-start = (bf16[128,1024]{1,0:T(8,128)(2,1)S(1)}, bf16[128,1024]{1,0:T(8,128)(2,1)S(1)}, u32[]{:S(2)}, u32[]{:S(2)}) collective-permute-start(bf16[128,1024]{1,0:T(8,128)(2,1)S(1)} %get-tuple-element.653), channel_id=1, source_target_pairs={{0,4},{4,8},{8,12},{12,16},{16,20},{20,24},{24,28},{28,32},{32,36}... | collective-permute-start | bytes 786440 | tf_op jit(solution)/shard_map/while/body/eval_jaxpr/ppermute | solution.py:13
  393.7 9.5 %collective-permute-start = (bf16[128,1024]{1,0:T(8,128)(2,1)S(1)}, bf16[128,1024]{1,0:T(8,128)(2,1)S(1)}, u32[]{:S(2)}, u32[]{:S(2)}) collective-permute-start(bf16[128,1024]{1,0:T(8,128)(2,1)S(1)} %get-tuple-element.653), channel_id=1, source_target_pairs={{0,4},{4,8},{8,12},{12,16},{16,20},{20,24},{24,28},{28,32},{32,36}... | collective-permute-start | bytes 786440 | tf_op jit(solution)/shard_map/while/body/eval_jaxpr/ppermute | solution.py:13
  407.6 9.5 %collective-permute-start = (bf16[128,1024]{1,0:T(8,128)(2,1)S(1)}, bf16[128,1024]{1,0:T(8,128)(2,1)S(1)}, u32[]{:S(2)}, u32[]{:S(2)}) collective-permute-start(bf16[128,1024]{1,0:T(8,128)(2,1)S(1)} %get-tuple-element.653), channel_id=1, source_target_pairs={{0,4},{4,8},{8,12},{12,16},{16,20},{20,24},{24,28},{28,32},{32,36}... | collective-permute-start | bytes 786440 | tf_op jit(solution)/shard_map/while/body/eval_jaxpr/ppermute | solution.py:13
  421.5 9.5 %collective-permute-start = (bf16[128,1024]{1,0:T(8,128)(2,1)S(1)}, bf16[128,1024]{1,0:T(8,128)(2,1)S(1)}, u32[]{:S(2)}, u32[]{:S(2)}) collective-permute-start(bf16[128,1024]{1,0:T(8,128)(2,1)S(1)} %get-tuple-element.653), channel_id=1, source_target_pairs={{0,4},{4,8},{8,12},{12,16},{16,20},{20,24},{24,28},{28,32},{32,36}... | collective-permute-start | bytes 786440 | tf_op jit(solution)/shard_map/while/body/eval_jaxpr/ppermute | solution.py:13
  435.5 9.5 %collective-permute-start = (bf16[128,1024]{1,0:T(8,128)(2,1)S(1)}, bf16[128,1024]{1,0:T(8,128)(2,1)S(1)}, u32[]{:S(2)}, u32[]{:S(2)}) collective-permute-start(bf16[128,1024]{1,0:T(8,128)(2,1)S(1)} %get-tuple-element.653), channel_id=1, source_target_pairs={{0,4},{4,8},{8,12},{12,16},{16,20},{20,24},{24,28},{28,32},{32,36}... | collective-permute-start | bytes 786440 | tf_op jit(solution)/shard_map/while/body/eval_jaxpr/ppermute | solution.py:13
  449.4 9.5 %collective-permute-start = (bf16[128,1024]{1,0:T(8,128)(2,1)S(1)}, bf16[128,1024]{1,0:T(8,128)(2,1)S(1)}, u32[]{:S(2)}, u32[]{:S(2)}) collective-permute-start(bf16[128,1024]{1,0:T(8,128)(2,1)S(1)} %get-tuple-element.653), channel_id=1, source_target_pairs={{0,4},{4,8},{8,12},{12,16},{16,20},{20,24},{24,28},{28,32},{32,36}... | collective-permute-start | bytes 786440 | tf_op jit(solution)/shard_map/while/body/eval_jaxpr/ppermute | solution.py:13
  463.3 9.5 %collective-permute-start = (bf16[128,1024]{1,0:T(8,128)(2,1)S(1)}, bf16[128,1024]{1,0:T(8,128)(2,1)S(1)}, u32[]{:S(2)}, u32[]{:S(2)}) collective-permute-start(bf16[128,1024]{1,0:T(8,128)(2,1)S(1)} %get-tuple-element.653), channel_id=1, source_target_pairs={{0,4},{4,8},{8,12},{12,16},{16,20},{20,24},{24,28},{28,32},{32,36}... | collective-permute-start | bytes 786440 | tf_op jit(solution)/shard_map/while/body/eval_jaxpr/ppermute | solution.py:13
  477.2 9.5 %collective-permute-start = (bf16[128,1024]{1,0:T(8,128)(2,1)S(1)}, bf16[128,1024]{1,0:T(8,128)(2,1)S(1)}, u32[]{:S(2)}, u32[]{:S(2)}) collective-permute-start(bf16[128,1024]{1,0:T(8,128)(2,1)S(1)} %get-tuple-element.653), channel_id=1, source_target_pairs={{0,4},{4,8},{8,12},{12,16},{16,20},{20,24},{24,28},{28,32},{32,36}... | collective-permute-start | bytes 786440 | tf_op jit(solution)/shard_map/while/body/eval_jaxpr/ppermute | solution.py:13
  491.1 9.5 %collective-permute-start = (bf16[128,1024]{1,0:T(8,128)(2,1)S(1)}, bf16[128,1024]{1,0:T(8,128)(2,1)S(1)}, u32[]{:S(2)}, u32[]{:S(2)}) collective-permute-start(bf16[128,1024]{1,0:T(8,128)(2,1)S(1)} %get-tuple-element.653), channel_id=1, source_target_pairs={{0,4},{4,8},{8,12},{12,16},{16,20},{20,24},{24,28},{28,32},{32,36}... | collective-permute-start | bytes 786440 | tf_op jit(solution)/shard_map/while/body/eval_jaxpr/ppermute | solution.py:13
  505.0 9.5 %collective-permute-start = (bf16[128,1024]{1,0:T(8,128)(2,1)S(1)}, bf16[128,1024]{1,0:T(8,128)(2,1)S(1)}, u32[]{:S(2)}, u32[]{:S(2)}) collective-permute-start(bf16[128,1024]{1,0:T(8,128)(2,1)S(1)} %get-tuple-element.653), channel_id=1, source_target_pairs={{0,4},{4,8},{8,12},{12,16},{16,20},{20,24},{24,28},{28,32},{32,36}... | collective-permute-start | bytes 786440 | tf_op jit(solution)/shard_map/while/body/eval_jaxpr/ppermute | solution.py:13
  519.0 9.5 %collective-permute-start = (bf16[128,1024]{1,0:T(8,128)(2,1)S(1)}, bf16[128,1024]{1,0:T(8,128)(2,1)S(1)}, u32[]{:S(2)}, u32[]{:S(2)}) collective-permute-start(bf16[128,1024]{1,0:T(8,128)(2,1)S(1)} %get-tuple-element.653), channel_id=1, source_target_pairs={{0,4},{4,8},{8,12},{12,16},{16,20},{20,24},{24,28},{28,32},{32,36}... | collective-permute-start | bytes 786440 | tf_op jit(solution)/shard_map/while/body/eval_jaxpr/ppermute | solution.py:13
  560.7 9.5 %collective-permute-start = (bf16[128,1024]{1,0:T(8,128)(2,1)S(1)}, bf16[128,1024]{1,0:T(8,128)(2,1)S(1)}, u32[]{:S(2)}, u32[]{:S(2)}) collective-permute-start(bf16[128,1024]{1,0:T(8,128)(2,1)S(1)} %get-tuple-element.653), channel_id=1, source_target_pairs={{0,4},{4,8},{8,12},{12,16},{16,20},{20,24},{24,28},{28,32},{32,36}... | collective-permute-start | bytes 786440 | tf_op jit(solution)/shard_map/while/body/eval_jaxpr/ppermute | solution.py:13
  659.5 17.2 %all-to-all-start = ((f32[32,1,128]{2,1,0:T(1,128)}), f32[32,1,128]{2,1,0:T(1,128)S(1)}, u32[]{:S(2)}, u32[]{:S(2)}) async-start(f32[32,1,128]{2,1,0:T(1,128)} %bitcast.8), calls=%async_computation.1 | async-start | bytes 32768 | tf_op jit(solution)/shard_map/all_to_all | solution.py:126
  676.7 13.4 %all-to-all-start.1 = ((f32[32,1,128]{2,1,0:T(1,128)}), f32[32,1,128]{2,1,0:T(1,128)S(1)}, u32[]{:S(2)}, u32[]{:S(2)}) async-start(f32[32,1,128]{2,1,0:T(1,128)} %bitcast.9), calls=%async_computation.2 | async-start | bytes 32768 | tf_op jit(solution)/shard_map/all_to_all | solution.py:127
  (6 other events, 102.7 us)
Sparse Core Ops, SparseCore 0:
  24.6 53.4 reduce-scatter.1
  81.8 53.8 all-gather.5
where the time goes:
time: 717 us; the launch traced here: 714 us
  waiting for transfers between devices  416 us (58%)
  blocking collectives  112 us (16%)
  local copies, waits for them, and re-layouts  88.7 us (12%)
  matrix products  54 us (8%)
  between operations  14.8 us (2%)
  starting transfers between devices  13.8 us (2%)
  other arithmetic  13.1 us (2%)
    ppermute x31, waiting for transfers between devices, from_behind(): return lax.ppermute(value, axis, pairs)  291 us
    all_gather x3, blocking collectives, combined_all(): gathered = jax.tree.map(lambda a: lax.all_gather(a, axis), part)  84.8 us
    reduce_scatter x1, waiting for transfers between devices, on_device(): lax.psum_scatter(lax.cond(is_image, lambda: project_rows(image_feats, ima...  53.6 us
    all_gather x1, waiting for transfers between devices, on_device(): joined = lax.all_gather(embedded, ('tower', 'mp'), axis=0, tiled=True)  53.4 us
    dot_general x32, matrix products, tile_stats(): lax.dot_general(text_block, images, (((1,), (1,)), ((), ())), preferred_e...  50.8 us
    dynamic_update_slice x31, local copies, waits for them, and re-layouts, advance(): lax.dynamic_update_slice(stored_sum, block_sum[None, :], (source, 0))  40 us
    dynamic_update_slice x31, local copies, waits for them, and re-layouts, advance(): lax.dynamic_update_slice(stored_max, block_max[None, :], (source, 0))  39.5 us
    all_gather x1, blocking collectives, on_device(): lax.all_gather(caption_loss, ('tower', 'mp'), axis=0, tiled=True)  16.5 us
  transfers between devices with their start and end apart: 35, of which 35 were waited for; matrix products, arithmetic and copies ran while one was open for 0% of the time, Pallas kernels for 0%

commit v1 on v0

v1 whole, which is shorter than its diff:
```python
import jax
import jax.numpy as jnp
from jax import lax
from jax.experimental import pallas as pl
from jax.experimental.pallas import tpu as pltpu
from jax.sharding import PartitionSpec as P

MESH = pl.DeviceIdType.MESH
F32 = jnp.float32
BF16 = jnp.bfloat16
ROWS = 1024
EMB = 1024
WIDTH = (5120, 1280)
LOCAL = (1280, 320)
PIECE = 128
HALF = 64
QUART = 32
NSEM = 160
LOW = -1e30


def wrap(value, count):
    return lax.rem(value + count, count)


def kernel(
    imf, txf, wim, wtx, scale_ref, pairs_ref, out_img, out_txt,
    xi, xt, wi, wt, mus, pf, pb, misc_send, misc_recv, relay, comb, fin, turn,
    img, txt, rmax, rsum, cmax, csum, rsend, rrecv, csend, crecv, fsend, frecv,
    lsem, ssem, rsem,
):
    tw = lax.axis_index("tower")
    blk = lax.axis_index("blk")
    x = lax.axis_index("mp")
    core = lax.rem(blk, 2)
    yh = lax.rem(blk // 2, 2)
    z = blk // 4
    y = yh * 2 + tw
    piece = tw * 4 + x

    def device(dx, dy, dz, dc):
        px = wrap(x + dx, 4)
        py = wrap(y + dy, 4)
        pz = wrap(z + dz, 8)
        pc = lax.rem(core + dc, 2)
        return {"tower": lax.rem(py, 2), "blk": (pz * 2 + py // 2) * 2 + pc, "mp": px}

    sent = []

    def send(src, dst, where):
        k = len(sent)
        copy = pltpu.make_async_remote_copy(
            src_ref=src, dst_ref=dst, send_sem=ssem.at[k], recv_sem=rsem.at[k],
            device_id=device(*where), device_id_type=MESH,
        )
        copy.start()
        sent.append(copy)
        return k

    def arrive(k, ref):
        pltpu.make_async_remote_copy(
            src_ref=ref, dst_ref=ref, send_sem=ssem.at[k], recv_sem=rsem.at[k],
            device_id=device(1, 0, 0, 0), device_id_type=MESH,
        ).wait_recv()

    half_rows = pl.ds(pl.multiple_of(tw * 512, 512), 512)
    loads = [
        pltpu.make_async_copy(imf.at[half_rows, :], xi, lsem.at[0]),
        pltpu.make_async_copy(wim, wi, lsem.at[1]),
        pltpu.make_async_copy(txf.at[half_rows, :], xt, lsem.at[2]),
        pltpu.make_async_copy(wtx, wt, lsem.at[3]),
    ]
    for load in loads:
        load.start()

    plane = [(dx, dy, 0, 0) for dy in range(4) for dx in range(4) if (dx, dy) != (0, 0)]
    column = [(0, 0, dz, dc) for dz in range(8) for dc in range(2) if (dz, dc) != (0, 0)]
    barrier = pltpu.get_barrier_semaphore()
    for where in plane + column:
        pl.semaphore_signal(barrier, inc=1, device_id=device(*where), device_id_type=MESH)

    lane = lax.broadcasted_iota(jnp.int32, (PIECE, PIECE), 1)

    def project(q, feats, weights):
        width = LOCAL[q]

        def rows_stats(d, carry):
            rows = pl.ds(pl.multiple_of(d * PIECE, PIECE), PIECE)
            values = feats[rows, :].astype(F32)
            first = jnp.sum(values, axis=1, keepdims=True)
            second = jnp.sum(values * values, axis=1, keepdims=True)
            mus[q, rows, :] = first / width
            flat = jnp.where(lane == 0, first, jnp.where(lane == 1, second, 0.0)).T
            misc_send[q, d, :, EMB : EMB + 128] = flat[0:1, :]
            misc_send[q, d, :, EMB + 128 : EMB + 256] = flat[1:2, :]
            return carry

        lax.fori_loop(0, 4, rows_stats, 0)

        def columns_step(n, carry):
            cols = pl.ds(pl.multiple_of(n * 256, 256), 256)
            block = weights[:, cols]
            total = jnp.dot(jnp.ones((8, width), BF16), block, preferred_element_type=F32)[0:1, :]
            part = jnp.dot(feats[...], block, preferred_element_type=F32) - mus[q] * total
            pf[q, :, cols] = part
            pb[q, :, cols] = part.astype(BF16)
            for d in range(4):
                misc_send[q, d, :, cols] = total
            return carry

        lax.fori_loop(0, 4, columns_step, 0)

    right, left, opposite = wrap(x + 1, 4), wrap(x + 3, 4), wrap(x + 2, 4)

    def part_rows(owner, start, count):
        return pl.ds(pl.multiple_of(owner * PIECE + start, HALF), count)

    def scatter_first(q):
        keys = {}
        keys["relay0"] = send(pb.at[q, part_rows(opposite, 0, HALF), :], relay.at[q, 0], (1, 0, 0, 0))
        keys["relay1"] = send(pb.at[q, part_rows(opposite, HALF, HALF), :], relay.at[q, 1], (3, 0, 0, 0))
        keys["fin0b"] = send(
            pb.at[q, part_rows(right, HALF, HALF), :], fin.at[q, 0, pl.ds(HALF, HALF), :], (1, 0, 0, 0)
        )
        keys["fin1a"] = send(
            pb.at[q, part_rows(left, 0, HALF), :], fin.at[q, 1, pl.ds(0, HALF), :], (3, 0, 0, 0)
        )
        keys["misc"] = [
            send(misc_send.at[q, wrap(x + d, 4)], misc_recv.at[q, x], (d, 0, 0, 0)) for d in (1, 3, 2)
        ]
        return keys

    def scatter_second(q, keys):
        arrive(keys["relay0"], relay.at[q, 0])
        comb[q, 0] = (pf[q, part_rows(right, 0, HALF), :] + relay[q, 0].astype(F32)).astype(BF16)
        keys["fin0a"] = send(comb.at[q, 0], fin.at[q, 0, pl.ds(0, HALF), :], (1, 0, 0, 0))
        arrive(keys["relay1"], relay.at[q, 1])
        comb[q, 1] = (pf[q, part_rows(left, HALF, HALF), :] + relay[q, 1].astype(F32)).astype(BF16)
        keys["fin1b"] = send(comb.at[q, 1], fin.at[q, 1, pl.ds(HALF, HALF), :], (3, 0, 0, 0))

    def finish(q, keys):
        for d, k in zip((1, 3, 2), keys["misc"]):
            arrive(k, misc_recv.at[q, wrap(x - d, 4)])
        misc_recv[q, x] = misc_send[q, x]
        turn[...] = jnp.zeros_like(turn)
        first = [misc_recv[q, s, :, EMB : EMB + 128] for s in range(4)]
        second = [misc_recv[q, s, :, EMB + 128 : EMB + 256] for s in range(4)]
        mean = (first[0] + first[1] + first[2] + first[3]) / WIDTH[q]
        square = (second[0] + second[1] + second[2] + second[3]) / WIDTH[q]
        turn[4:5, :] = lax.rsqrt(square - mean * mean + 1e-06)
        for s in range(4):
            turn[s : s + 1, :] = first[s] / LOCAL[q] - mean
        columns = turn[...].T
        arrive(keys["fin0b"], fin.at[q, 0, pl.ds(HALF, HALF), :])
        arrive(keys["fin1a"], fin.at[q, 1, pl.ds(0, HALF), :])
        arrive(keys["fin0a"], fin.at[q, 0, pl.ds(0, HALF), :])
        arrive(keys["fin1b"], fin.at[q, 1, pl.ds(HALF, HALF), :])
        total = pf[q, part_rows(x, 0, PIECE), :] + fin[q, 0].astype(F32) + fin[q, 1].astype(F32)
        for s in range(4):
            total = total + columns[:, s : s + 1] * misc_recv[q, s, :, 0:EMB]
        projected = total * columns[:, 4:5]
        length = lax.rsqrt(jnp.sum(projected * projected, axis=1, keepdims=True) + 1e-06)
        return (projected * length).astype(BF16)

    loads[0].wait()
    loads[1].wait()
    project(0, xi, wi)
    pl.semaphore_wait(barrier, len(plane) + len(column))
    keys0 = scatter_first(0)
    loads[2].wait()
    loads[3].wait()
    project(1, xt, wt)
    keys1 = scatter_first(1)
    rmax[...] = jnp.full(rmax.shape, LOW, F32)
    rsum[...] = jnp.zeros(rsum.shape, F32)
    cmax[...] = jnp.full(cmax.shape, LOW, F32)
    csum[...] = jnp.zeros(csum.shape, F32)
    scatter_second(0, keys0)
    scatter_second(1, keys1)

    def unit_a(dx, dy):
        return wrap(y + dy, 4), wrap(x + dx, 4)

    def unit_b(dx, dy):
        return 4 + wrap(x + dx, 4), wrap(y + dy, 4)

    def chunk(pair, start=0, count=HALF):
        unit, place = pair
        return img.at[unit, pl.ds(pl.multiple_of(place * HALF + start, QUART), count), :]

    MOVE = {"x": lambda s: (s, 0, 0, 0), "y": lambda s: (0, s, 0, 0)}

    def spread(axis, ref):
        return [send(ref, ref, MOVE[axis](1)), send(ref, ref, MOVE[axis](3))]

    def pass_on(axis, keys, lower, upper):
        arrive(keys[0], chunk(lower))
        low = send(chunk(lower, 0, QUART), chunk(lower, 0, QUART), MOVE[axis](1))
        arrive(keys[1], chunk(upper))
        high = send(chunk(upper, QUART, QUART), chunk(upper, QUART, QUART), MOVE[axis](3))
        return low, high

    def land(keys, far):
        arrive(keys[0], chunk(far, 0, QUART))
        arrive(keys[1], chunk(far, QUART, QUART))

    emb_img = finish(0, keys0)
    own_a, own_b = unit_a(0, 0), unit_b(0, 0)
    img[own_a[0], pl.ds(pl.multiple_of(own_a[1] * HALF, HALF), HALF), :] = emb_img[0:HALF]
    img[own_b[0], pl.ds(pl.multiple_of(own_b[1] * HALF, HALF), HALF), :] = emb_img[HALF:PIECE]
    a_x = spread("x", chunk(own_a))
    b_y = spread("y", chunk(own_b))
    a_y = {0: spread("y", chunk(own_a))}
    b_x = {0: spread("x", chunk(own_b))}

    def cap(dz, other=0, start=0, count=PIECE):
        place = lax.rem(core + other, 2) * PIECE
        return txt.at[wrap(z + dz, 8), pl.ds(pl.multiple_of(place + start, HALF), count), :]

    emb_txt = finish(1, keys1)
    txt[z, pl.ds(pl.multiple_of(core * PIECE, PIECE), PIECE), :] = emb_txt
    up = {1: send(cap(0), cap(0), (0, 0, 1, 0))}
    down = {1: send(cap(0), cap(0), (0, 0, 7, 0))}
    pair_keys = {0: send(cap(0), cap(0), (0, 0, 0, 1))}

    def captions_step(d):
        if d < 4:
            arrive(up[d], cap(-d))
            if d < 3:
                up[d + 1] = send(cap(-d), cap(-d), (0, 0, 1, 0))
            else:
                up[4] = send(cap(-3, 0, 0, HALF), cap(-3, 0, 0, HALF), (0, 0, 1, 0))
            pair_keys[-d] = send(cap(-d), cap(-d), (0, 0, 0, 1))
            arrive(down[d], cap(d))
            if d < 3:
                down[d + 1] = send(cap(d), cap(d), (0, 0, 7, 0))
            else:
                down[4] = send(cap(3, 0, HALF, HALF), cap(3, 0, HALF, HALF), (0, 0, 7, 0))
            pair_keys[d] = send(cap(d), cap(d), (0, 0, 0, 1))
        else:
            arrive(up[4], cap(4, 0, 0, HALF))
            arrive(down[4], cap(4, 0, HALF, HALF))
            pair_keys[4] = send(cap(4), cap(4), (0, 0, 0, 1))

    scale = scale_ref[0, 0]

    def signed(k):
        return ((k + 1) // 2) * (1 - 2 * lax.rem(k + 1, 2))

    def tile(j, k):
        kind = lax.rem(j, 2)
        unit = kind * 4 + wrap((1 - kind) * y + kind * x + signed(j // 2), 4)
        column_unit = wrap(z + signed(k), 8)
        scores = scale * lax.dot_general(
            img[unit], txt[column_unit], (((1,), (1,)), ((), ())), preferred_element_type=F32
        )
        top = jnp.max(scores, axis=1, keepdims=True)
        total = jnp.sum(jnp.exp(scores - top), axis=1, keepdims=True)
        old = rmax[unit]
        new = jnp.maximum(old, top)
        rsum[unit] = rsum[unit] * jnp.exp(old - new) + total * jnp.exp(top - new)
        rmax[unit] = new
        top = jnp.max(scores, axis=0, keepdims=True)
        total = jnp.sum(jnp.exp(scores - top), axis=0, keepdims=True)
        old = cmax[column_unit]
        new = jnp.maximum(old, top)
        csum[column_unit] = csum[column_unit] * jnp.exp(old - new) + total * jnp.exp(top - new)
        cmax[column_unit] = new

    def wave(j0, j1, k0, k1):
        span = k1 - k0

        def step(i, carry):
            tile(j0 + i // span, k0 + lax.rem(i, span))
            return carry

        lax.fori_loop(0, (j1 - j0) * span, step, 0)

    def sibling(dz):
        arrive(pair_keys[dz], cap(dz, 1))

    a_far, b_far = {}, {}
    a_x_far = pass_on("x", a_x, unit_a(-1, 0), unit_a(1, 0))
    b_y_far = pass_on("y", b_y, unit_b(0, -1), unit_b(0, 1))
    for s in (-1, 1):
        a_y[s] = spread("y", chunk(unit_a(s, 0)))
        b_x[s] = spread("x", chunk(unit_b(0, s)))
    a_far[0] = pass_on("y", a_y[0], unit_a(0, -1), unit_a(0, 1))
    b_far[0] = pass_on("x", b_x[0], unit_b(-1, 0), unit_b(1, 0))
    land(a_x_far, unit_a(2, 0))
    land(b_y_far, unit_b(0, 2))
    a_y[2] = spread("y", chunk(unit_a(2, 0)))
    b_x[2] = spread("x", chunk(unit_b(0, 2)))
    captions_step(1)
    sibling(0)
    wave(0, 2, 0, 1)
    for s in (-1, 1):
        a_far[s] = pass_on("y", a_y[s], unit_a(s, -1), unit_a(s, 1))
        b_far[s] = pass_on("x", b_x[s], unit_b(-1, s), unit_b(1, s))
    sibling(-1)
    sibling(1)
    wave(0, 2, 1, 3)
    captions_step(2)
    a_far[2] = pass_on("y", a_y[2], unit_a(2, -1), unit_a(2, 1))
    b_far[2] = pass_on("x", b_x[2], unit_b(-1, 2), unit_b(1, 2))
    wave(2, 6, 0, 3)
    sibling(-2)
    sibling(2)
    captions_step(3)
    wave(0, 6, 3, 5)

    sibling(-3)
    sibling(3)
    wave(0, 6, 5, 7)
    captions_step(4)
    for s in (0, -1, 1, 2):
        land(a_far[s], unit_a(s, 2))
        land(b_far[s], unit_b(2, s))
    own_caps = txt[z, pl.ds(pl.multiple_of(core * PIECE, PIECE), PIECE), :]
    turn[...] = jnp.zeros_like(turn)
    turn[0:8, :] = pairs_ref[...].astype(F32)
    partner = turn[...].T
    mine = (piece * PIECE + lane).astype(F32)
    caption_positive = jnp.zeros((1, PIECE), F32)
    image_positive = jnp.zeros((PIECE, PIECE), F32)
    for p in range(8):
        t, px = p // 4, p % 4
        rows = jnp.concatenate(
            [
                img[yh * 2 + t, px * HALF : (px + 1) * HALF, :],
                img[4 + px, pl.ds(pl.multiple_of((yh * 2 + t) * HALF, HALF), HALF), :],
            ],
            axis=0,
        )
        scores = scale * lax.dot_general(
            rows, own_caps, (((1,), (1,)), ((), ())), preferred_element_type=F32
        )
        picked = jnp.where(partner[:, p : p + 1] == mine, scores, 0.0)
        caption_positive = caption_positive + jnp.sum(picked, axis=0, keepdims=True)
        image_positive = jnp.where(lane == p, jnp.sum(picked, axis=1, keepdims=True), image_positive)
    image_positive = image_positive.T

    wave(6, 8, 0, 7)
    sibling(4)
    wave(0, 8, 7, 8)

    for u in range(8):
        logs = cmax[u] + jnp.log(csum[u])
        csend[2 * u] = logs[:, 0:PIECE]
        csend[2 * u + 1] = logs[:, PIECE : 2 * PIECE]
    me_column = z * 2 + core
    column_keys = []
    for where in column:
        target = wrap(z + where[2], 8) * 2 + lax.rem(core + where[3], 2)
        column_keys.append(send(csend.at[target], crecv.at[me_column], where))
    wide = lax.broadcasted_iota(jnp.int32, (256, PIECE), 1)
    logs = jnp.zeros((256, PIECE), F32)
    for u in range(8):
        logs = jnp.where(wide == u, rmax[u] + jnp.log(rsum[u]), logs)
    logs_low, logs_high = logs[0:PIECE].T, logs[PIECE:256].T
    parts = [logs_low, logs_high]

    def quarter(u, place):
        return parts[place // 2][u : u + 1, (place % 2) * HALF : (place % 2 + 1) * HALF]

    same = [(yh == 0).astype(F32), (yh == 1).astype(F32)]
    for py in range(4):
        for px in range(4):
            rsend[py * 4 + px, 0:1, :] = jnp.concatenate([quarter(py, px), quarter(4 + px, py)], axis=1)
            p = (py % 2) * 4 + px
            rsend[py * 4 + px, 1:2, :] = image_positive[p : p + 1, :] * same[py // 2]
    me_plane = y * 4 + x
    plane_keys = []
    for where in plane:
        target = wrap(y + where[1], 4) * 4 + wrap(x + where[0], 4)
        plane_keys.append(send(rsend.at[target], rrecv.at[me_plane], where))
    crecv[me_column] = csend[me_column]
    rrecv[me_plane] = rsend[me_plane]
    for where, k in zip(column, column_keys):
        source = wrap(z - where[2], 8) * 2 + lax.rem(core + where[3], 2)
        arrive(k, crecv.at[source])
    for where, k in zip(plane, plane_keys):
        source = wrap(y - where[1], 4) * 4 + wrap(x - where[0], 4)
        arrive(k, rrecv.at[source])

    def merge(rows):
        top = jnp.max(rows, axis=0)
        return top + jnp.log(jnp.sum(jnp.exp(rows - top[None]), axis=0))

    image_rows = rrecv[...]
    fsend[0:1, :] = merge(image_rows[:, 0:1, :]) - jnp.sum(image_rows[:, 1:2, :], axis=0)
    fsend[1:2, :] = merge(crecv[...]) - caption_positive
    shard = [(dx, dt) for dt in range(2) for dx in range(4) if (dx, dt) != (0, 0)]
    shard_keys = []
    step_y = [0, 1 - 2 * tw]
    for dx, dt in shard:
        shard_keys.append(send(fsend, frecv.at[piece], (dx, step_y[dt], 0, 0)))
    frecv[piece] = fsend[...]
    for (dx, dt), k in zip(shard, shard_keys):
        source = lax.rem(tw + dt, 2) * 4 + wrap(x - dx, 4)
        arrive(k, frecv.at[source])
    for p in range(8):
        out_img[p : p + 1, :] = frecv[p, 0:1, :]
        out_txt[p : p + 1, :] = frecv[p, 1:2, :]
    for copy in sent:
        copy.wait_send()


def on_device(image_feats, text_feats, image_proj, text_proj, logit_scale, pairs):
    vmem = pl.BlockSpec(memory_space=pltpu.VMEM)
    hbm = pl.BlockSpec(memory_space=pl.ANY)
    out = jax.ShapeDtypeStruct((8, 128), F32)
    image_loss, text_loss = pl.pallas_call(
        kernel,
        out_shape=(out, out),
        in_specs=[hbm, hbm, hbm, hbm, pl.BlockSpec(memory_space=pltpu.SMEM), vmem],
        out_specs=(vmem, vmem),
        scratch_shapes=[
            pltpu.VMEM((512, LOCAL[0]), BF16),
            pltpu.VMEM((512, LOCAL[1]), BF16),
            pltpu.VMEM((LOCAL[0], EMB), BF16),
            pltpu.VMEM((LOCAL[1], EMB), BF16),
            pltpu.VMEM((2, 512, 1), F32),
            pltpu.VMEM((2, 512, EMB), F32),
            pltpu.VMEM((2, 512, EMB), BF16),
            pltpu.VMEM((2, 4, 1, EMB + 256), F32),
            pltpu.VMEM((2, 4, 1, EMB + 256), F32),
            pltpu.VMEM((2, 2, HALF, EMB), BF16),
            pltpu.VMEM((2, 2, HALF, EMB), BF16),
            pltpu.VMEM((2, 2, PIECE, EMB), BF16),
            pltpu.VMEM((PIECE, PIECE), F32),
            pltpu.VMEM((8, 256, EMB), BF16),
            pltpu.VMEM((8, 256, EMB), BF16),
            pltpu.VMEM((8, 256, 1), F32),
            pltpu.VMEM((8, 256, 1), F32),
            pltpu.VMEM((8, 1, 256), F32),
            pltpu.VMEM((8, 1, 256), F32),
            pltpu.VMEM((16, 2, PIECE), F32),
            pltpu.VMEM((16, 2, PIECE), F32),
            pltpu.VMEM((16, 1, PIECE), F32),
            pltpu.VMEM((16, 1, PIECE), F32),
            pltpu.VMEM((2, PIECE), F32),
            pltpu.VMEM((8, 2, PIECE), F32),
            pltpu.SemaphoreType.DMA((4,)),
            pltpu.SemaphoreType.DMA((NSEM,)),
            pltpu.SemaphoreType.DMA((NSEM,)),
        ],
        compiler_params=pltpu.CompilerParams(
            collective_id=0, has_side_effects=True, vmem_limit_bytes=60 * 1024 * 1024
        ),
    )(
        image_feats, text_feats, image_proj, text_proj,
        logit_scale.reshape(1, 1), pairs.reshape(8, 128),
    )
    return (image_loss.reshape(ROWS), text_loss.reshape(ROWS))


def solution(mesh):
    return jax.shard_map(
        on_device,
        mesh=mesh,
        in_specs=(
            P("blk", "mp"),
            P("blk", "mp"),
            P("mp", None),
            P("mp", None),
            P(),
            P("blk", None),
        ),
        out_specs=(P("blk"), P("blk")),
        check_vma=False,
    )
```

time: 717 us -> 99.8 us (0.14)
  waiting for transfers between devices: 416 us -> 0 us
  blocking collectives: 112 us -> 0 us
  Pallas kernels: 0 us -> 93.4 us
  local copies, waits for them, and re-layouts: 88.7 us -> 4.78 us
  matrix products: 54 us -> 0 us
  starting transfers between devices: 13.8 us -> 0 us
  between operations: 14.8 us -> 1.29 us
  other arithmetic: 13.1 us -> 0 us
    ppermute x31 -> x0, waiting for transfers between devices: 291 us -> none  [from_behind(): return lax.ppermute(value, axis, pairs)]
    all_gather x4 -> x0, blocking collectives: 101 us -> none  [the longest x3 84.8 us: combined_all(): gathered = jax.tree.map(lambda a: lax.all_gather(a, axis), part)]
    pallas_call x0 -> x1, Pallas kernels: none -> 93.4 us  [on_device(): pl.pallas_call(kernel, out_shape=(out, out), in_specs=[hbm, hbm, hbm, hbm...]
    dynamic_update_slice x64 -> x0, local copies, waits for them, and re-layouts: 82.1 us -> none  [the longest x31 40 us: advance(): lax.dynamic_update_slice(stored_sum, block_sum[None, :], (source, 0))]
    dot_general x33 -> x0, matrix products: 54 us -> none  [the longest x32 50.8 us: tile_stats(): lax.dot_general(text_block, images, (((1,), (1,)), ((), ())), preferred_e...]
    reduce_scatter x1 -> x0, waiting for transfers between devices: 53.6 us -> none  [on_device(): lax.psum_scatter(lax.cond(is_image, lambda: project_rows(image_feats, ima...]
    all_gather x1 -> x0, waiting for transfers between devices: 53.4 us -> none  [on_device(): joined = lax.all_gather(embedded, ('tower', 'mp'), axis=0, tiled=True)]
    all_to_all x2 -> x0, waiting for transfers between devices: 18.1 us -> none  [the longest x1 9.15 us: on_device(): lax.all_to_all(slot_max, 'blk', split_axis=0, concat_axis=0, tiled=True)]
  transfers between devices with their start and end apart: 35 -> 0, of which waited for: 35 -> 0; matrix products, arithmetic and copies ran while one was open for 0% -> 0% of each run, Pallas kernels for 0% -> 0%
where the time goes in v1:
time: 99.8 us; the launch traced here: 99.5 us
  Pallas kernels  93.4 us (94%)
  local copies, waits for them, and re-layouts  4.78 us (5%)
  between operations  1.29 us (1%)
    pallas_call x1, Pallas kernels, on_device(): pl.pallas_call(kernel, out_shape=(out, out), in_specs=[hbm, hbm, hbm, hbm...  93.4 us
    unnamed x3, local copies, waits for them, and re-layouts  4.78 us

profile of v1, /device:TPU:8, one launch (start us, length us, event | category | flops | bytes accessed | tf_op | source)
XLA Modules:
  0.0 99.5 jit_solution(12446504511509549112)
XLA Ops:
  1.3 2.2 %copy.8.txf = bf16[1024,320]{1,0:T(8,128)(2,1)} copy(bf16[1024,320]{0,1:T(8,128)(2,1)} %param.7) | data formatting | bytes 1310720 | tf_op args[1]
  3.5 93.4 %shard_map.77 = (f32[8,128]{1,0:T(8,128)}, f32[8,128]{1,0:T(8,128)}) custom-call(bf16[1024,1280]{1,0:T(8,128)(2,1)} %imf.1, bf16[1024,320]{1,0:T(8,128)(2,1)} %copy.8.txf, bf16[1280,1024]{1,0:T(8,128)(2,1)} %wim.1, bf16[320,1024]{1,0:T(8,128)(2,1)} %wtx.1, f32[1,1]{1,0:T(1,128)} %bitcast.4.scale_ref, s32[8,128]{1,0:T(8,128)} %bitcast.5), custom_call_target="tpu_custom_call" | custom-call | tf_op jit(solution)/shard_map/pallas_call | solution.py:413
  97.0 1.3 %copy.12 = f32[1024]{0:T(1024)} copy(f32[1024]{0:T(1024)} %bitcast.7) | data formatting | bytes 8192
  98.2 1.3 %copy.13 = f32[1024]{0:T(1024)} copy(f32[1024]{0:T(1024)} %bitcast.6) | data formatting | bytes 8192

commit v2 on v1

v2 whole, which is shorter than its diff:
```python
import jax
import jax.numpy as jnp
from jax import lax
from jax.experimental import pallas as pl
from jax.experimental.pallas import tpu as pltpu
from jax.sharding import PartitionSpec as P

MESH = pl.DeviceIdType.MESH
F32 = jnp.float32
BF16 = jnp.bfloat16
ROWS = 1024
EMB = 1024
WIDTH = (5120, 1280)
LOCAL = (1280, 320)
PIECE = 128
HALF = 64
QUART = 32
NSEM = 160
NA, NB = 80, 48
CUT_A, CUT_B = 48, 16
LOG2E = 1.4426950408889634
LN2 = 0.6931471805599453
LOW = -1e30


def wrap(value, count):
    return lax.rem(value + count, count)


def kernel(
    imf, txf, wim, wtx, scale_ref, pairs_ref, out,
    xi, xt, wi, wt, mus, pf, pb, misc_send, misc_recv, relay, comb, fin, turn, columns,
    img_a, img_b, txt, rmax_a, rsum_a, rmax_b, rsum_b, cmax, csum,
    rsend, rrecv, csend, crecv, fsend, frecv, lsem, ssem, rsem,
):
    tw = lax.axis_index("tower")
    blk = lax.axis_index("blk")
    x = lax.axis_index("mp")
    core = lax.rem(blk, 2)
    yh = lax.rem(blk // 2, 2)
    z = blk // 4
    y = yh * 2 + tw
    piece = tw * 4 + x

    def device(dx, dy, dz, dc):
        px = wrap(x + dx, 4)
        py = wrap(y + dy, 4)
        pz = wrap(z + dz, 8)
        pc = lax.rem(core + dc, 2)
        return {"tower": lax.rem(py, 2), "blk": (pz * 2 + py // 2) * 2 + pc, "mp": px}

    sent = []

    def send(src, dst, where):
        k = len(sent)
        copy = pltpu.make_async_remote_copy(
            src_ref=src, dst_ref=dst, send_sem=ssem.at[k], recv_sem=rsem.at[k],
            device_id=device(*where), device_id_type=MESH,
        )
        copy.start()
        sent.append(copy)
        return k

    def arrive(k, ref):
        pltpu.make_async_remote_copy(
            src_ref=ref, dst_ref=ref, send_sem=ssem.at[k], recv_sem=rsem.at[k],
            device_id=device(1, 0, 0, 0), device_id_type=MESH,
        ).wait_recv()

    half_rows = pl.ds(pl.multiple_of(tw * 512, 512), 512)
    loads = [
        pltpu.make_async_copy(imf.at[half_rows, :], xi, lsem.at[0]),
        pltpu.make_async_copy(wim, wi, lsem.at[1]),
        pltpu.make_async_copy(txf.at[:, half_rows], xt, lsem.at[2]),
        pltpu.make_async_copy(wtx, wt, lsem.at[3]),
    ]
    for load in loads:
        load.start()

    plane = [(dx, dy, 0, 0) for dy in range(4) for dx in range(4) if (dx, dy) != (0, 0)]
    column = [(0, 0, dz, dc) for dz in range(8) for dc in range(2) if (dz, dc) != (0, 0)]
    barrier = pltpu.get_barrier_semaphore()
    for where in plane + column:
        pl.semaphore_signal(barrier, inc=1, device_id=device(*where), device_id_type=MESH)

    lane = lax.broadcasted_iota(jnp.int32, (PIECE, PIECE), 1)

    def project(q, feats, weights):
        width = LOCAL[q]

        def rows_stats(d, carry):
            rows = pl.ds(pl.multiple_of(d * PIECE, PIECE), PIECE)
            if q == 0:
                values = feats[rows, :].astype(F32)
                first = jnp.sum(values, axis=1, keepdims=True)
                second = jnp.sum(values * values, axis=1, keepdims=True)
                mus[q, rows, :] = first / width
                flat = jnp.where(lane == 0, first, jnp.where(lane == 1, second, 0.0)).T
                first, second = flat[0:1, :], flat[1:2, :]
            else:
                values = feats[:, rows].astype(F32)
                first = jnp.sum(values, axis=0, keepdims=True)
                second = jnp.sum(values * values, axis=0, keepdims=True)
                flat = jnp.broadcast_to(first / width, (PIECE, PIECE)).T
                mus[q, rows, :] = flat[:, 0:1]
            misc_send[q, d, :, EMB : EMB + 128] = first
            misc_send[q, d, :, EMB + 128 : EMB + 256] = second
            return carry

        lax.fori_loop(0, 4, rows_stats, 0)
        contract = (((1,), (0,)), ((), ())) if q == 0 else (((0,), (0,)), ((), ()))

        def columns_step(n, carry):
            cols = pl.ds(pl.multiple_of(n * 256, 256), 256)
            block = weights[:, cols]
            total = jnp.dot(jnp.ones((8, width), BF16), block, preferred_element_type=F32)[0:1, :]
            part = lax.dot_general(feats[...], block, contract, preferred_element_type=F32) - mus[q] * total
            pf[q, :, cols] = part
            pb[q, :, cols] = part.astype(BF16)
            for d in range(4):
                misc_send[q, d, :, cols] = total
            return carry

        lax.fori_loop(0, 4, columns_step, 0)

    right, left, opposite = wrap(x + 1, 4), wrap(x + 3, 4), wrap(x + 2, 4)

    def part_rows(owner, start, count):
        return pl.ds(pl.multiple_of(owner * PIECE + start, 16), count)

    def scatter_misc(q):
        return [send(misc_send.at[q, wrap(x + d, 4)], misc_recv.at[q, x], (d, 0, 0, 0)) for d in (1, 3, 2)]

    def scatter_first(q, start, count, cut):
        low, high = pl.ds(start, cut), pl.ds(start + cut, count - cut)
        return {
            "batch": (q, start, count, cut),
            "relay0": send(pb.at[q, part_rows(opposite, start, cut), :], relay.at[q, 0, low, :], (1, 0, 0, 0)),
            "relay1": send(
                pb.at[q, part_rows(opposite, start + cut, count - cut), :], relay.at[q, 1, high, :], (3, 0, 0, 0)
            ),
            "fin0b": send(
                pb.at[q, part_rows(right, start + cut, count - cut), :], fin.at[q, 0, high, :], (1, 0, 0, 0)
            ),
            "fin1a": send(pb.at[q, part_rows(left, start, cut), :], fin.at[q, 1, low, :], (3, 0, 0, 0)),
        }

    def scatter_second(keys):
        q, start, count, cut = keys["batch"]
        low, high = pl.ds(start, cut), pl.ds(start + cut, count - cut)
        arrive(keys["relay0"], relay.at[q, 0, low, :])
        comb[q, low, :] = (pf[q, part_rows(right, start, cut), :] + relay[q, 0, low, :].astype(F32)).astype(BF16)
        keys["fin0a"] = send(comb.at[q, low, :], fin.at[q, 0, low, :], (1, 0, 0, 0))
        arrive(keys["relay1"], relay.at[q, 1, high, :])
        comb[q, high, :] = (
            pf[q, part_rows(left, start + cut, count - cut), :] + relay[q, 1, high, :].astype(F32)
        ).astype(BF16)
        keys["fin1b"] = send(comb.at[q, high, :], fin.at[q, 1, high, :], (3, 0, 0, 0))

    def settle(q, keys):
        for d, k in zip((1, 3, 2), keys):
            arrive(k, misc_recv.at[q, wrap(x - d, 4)])
        misc_recv[q, x] = misc_send[q, x]
        turn[...] = jnp.zeros_like(turn)
        first = [misc_recv[q, s, :, EMB : EMB + 128] for s in range(4)]
        second = [misc_recv[q, s, :, EMB + 128 : EMB + 256] for s in range(4)]
        mean = (first[0] + first[1] + first[2] + first[3]) / WIDTH[q]
        square = (second[0] + second[1] + second[2] + second[3]) / WIDTH[q]
        turn[4:5, :] = lax.rsqrt(square - mean * mean + 1e-06)
        for s in range(4):
            turn[s : s + 1, :] = first[s] / LOCAL[q] - mean
        columns[q] = turn[...].T

    def finish(keys):
        q, start, count, cut = keys["batch"]
        low, high, rows = pl.ds(start, cut), pl.ds(start + cut, count - cut), pl.ds(start, count)
        arrive(keys["fin0b"], fin.at[q, 0, high, :])
        arrive(keys["fin1a"], fin.at[q, 1, low, :])
        arrive(keys["fin0a"], fin.at[q, 0, low, :])
        arrive(keys["fin1b"], fin.at[q, 1, high, :])
        total = pf[q, part_rows(x, start, count), :] + fin[q, 0, rows, :].astype(F32) + fin[q, 1, rows, :].astype(F32)
        for s in range(4):
            total = total + columns[q, rows, s : s + 1] * misc_recv[q, s, :, 0:EMB]
        projected = total * columns[q, rows, 4:5]
        length = lax.rsqrt(jnp.sum(projected * projected, axis=1, keepdims=True) + 1e-06)
        return (projected * length).astype(BF16)

    def unit_a(dx, dy):
        return img_a, NA, wrap(y + dy, 4), wrap(x + dx, 4)

    def unit_b(dx, dy):
        return img_b, NB, wrap(x + dx, 4), wrap(y + dy, 4)

    CUT = {NA: CUT_A, NB: CUT_B}

    def chunk(where, part=None):
        ref, size, unit, place = where
        start, count = {None: (0, size), 0: (0, CUT[size]), 1: (CUT[size], size - CUT[size])}[part]
        return ref.at[unit, pl.ds(pl.multiple_of(place * size + start, 16), count), :]

    move = {"x": lambda s: (s, 0, 0, 0), "y": lambda s: (0, s, 0, 0)}

    def spread(axis, where):
        ref = chunk(where)
        return [send(ref, ref, move[axis](1)), send(ref, ref, move[axis](3))]

    def pass_on(axis, keys, lower, upper):
        arrive(keys[0], chunk(lower))
        low = send(chunk(lower, 0), chunk(lower, 0), move[axis](1))
        arrive(keys[1], chunk(upper))
        high = send(chunk(upper, 1), chunk(upper, 1), move[axis](3))
        return low, high

    def land(keys, far):
        arrive(keys[0], chunk(far, 0))
        arrive(keys[1], chunk(far, 1))

    def store_image(where, rows):
        ref, size, unit, place = where
        ref[unit, pl.ds(pl.multiple_of(place * size, 16), size), :] = rows

    def cap(dz, half, other=0, start=0, count=HALF):
        place = lax.rem(core + other, 2) * PIECE + half * HALF
        return txt.at[wrap(z + dz, 8), pl.ds(pl.multiple_of(place + start, 16), count), :]

    up, down, pair_keys = {}, {}, {}

    def captions_start(half, rows):
        txt[z, pl.ds(pl.multiple_of(core * PIECE + half * HALF, HALF), HALF), :] = rows
        up[half, 1] = send(cap(0, half), cap(0, half), (0, 0, 1, 0))
        down[half, 1] = send(cap(0, half), cap(0, half), (0, 0, 7, 0))
        pair_keys[half, 0] = send(cap(0, half), cap(0, half), (0, 0, 0, 1))

    def captions_step(half, d):
        if d < 4:
            arrive(up[half, d], cap(-d, half))
            if d < 3:
                up[half, d + 1] = send(cap(-d, half), cap(-d, half), (0, 0, 1, 0))
            else:
                up[half, 4] = send(cap(-3, half, 0, 0, QUART), cap(-3, half, 0, 0, QUART), (0, 0, 1, 0))
            arrive(down[half, d], cap(d, half))
            if d < 3:
                down[half, d + 1] = send(cap(d, half), cap(d, half), (0, 0, 7, 0))
            else:
                down[half, 4] = send(cap(3, half, 0, QUART, QUART), cap(3, half, 0, QUART, QUART), (0, 0, 7, 0))
            pair_keys[half, -d] = send(cap(-d, half), cap(-d, half), (0, 0, 0, 1))
            pair_keys[half, d] = send(cap(d, half), cap(d, half), (0, 0, 0, 1))
        else:
            arrive(up[half, 4], cap(4, half, 0, 0, QUART))
            arrive(down[half, 4], cap(4, half, 0, QUART, QUART))
            pair_keys[half, 4] = send(cap(4, half), cap(4, half), (0, 0, 0, 1))

    def sibling(*offsets):
        for dz in offsets:
            for half in (0, 1):
                arrive(pair_keys[half, dz], cap(dz, half, 1))

    scale = scale_ref[0, 0]
    scale2 = scale * LOG2E

    def signed(k):
        if isinstance(k, int):
            return ((k + 1) // 2) * (1 - 2 * ((k + 1) % 2))
        return ((k + 1) // 2) * (1 - 2 * lax.rem(k + 1, 2))

    def update(max_ref, sum_ref, unit, top, total):
        old, held = max_ref[unit], sum_ref[unit]
        gap = old - top
        small = jnp.exp2(-jnp.abs(gap))
        keep = gap >= 0
        max_ref[unit] = jnp.maximum(old, top)
        sum_ref[unit] = jnp.where(keep, held, total) + jnp.where(keep, total, held) * small

    def group(images, max_ref, sum_ref, unit, ks):
        units = [wrap(z + signed(k), 8) for k in ks]
        scores = [
            scale2 * lax.dot_general(images[unit], txt[v], (((1,), (1,)), ((), ())), preferred_element_type=F32)
            for v in units
        ]
        for v, block in zip(units, scores):
            top = jnp.max(block, axis=0, keepdims=True)
            update(cmax, csum, v, top, jnp.sum(jnp.exp2(block - top), axis=0, keepdims=True))
        widest = scores[0]
        for block in scores[1:]:
            widest = jnp.maximum(widest, block)
        top = jnp.max(widest, axis=1, keepdims=True)
        total = jnp.exp2(scores[0] - top)
        for block in scores[1:]:
            total = total + jnp.exp2(block - top)
        update(max_ref, sum_ref, unit, top, jnp.sum(total, axis=1, keepdims=True))

    def wave(j0, j1, *ks):
        def step(j, carry):
            group(img_a, rmax_a, rsum_a, wrap(y + signed(j), 4), ks)
            group(img_b, rmax_b, rsum_b, wrap(x + signed(j), 4), ks)
            return carry

        lax.fori_loop(j0, j1, step, 0)

    loads[0].wait()
    loads[1].wait()
    project(0, xi, wi)
    pl.semaphore_wait(barrier, len(plane) + len(column))
    first_a = scatter_first(0, 0, NA, CUT_A)
    misc_image = scatter_misc(0)
    loads[2].wait()
    loads[3].wait()
    project(1, xt, wt)
    first_t0 = scatter_first(1, 0, HALF, QUART)
    misc_text = scatter_misc(1)
    for ref in (rmax_a, rmax_b, cmax):
        ref[...] = jnp.full(ref.shape, LOW, F32)
    for ref in (rsum_a, rsum_b, csum):
        ref[...] = jnp.zeros(ref.shape, F32)
    scatter_second(first_a)
    settle(0, misc_image)
    first_b = scatter_first(0, NA, NB, CUT_B)
    scatter_second(first_t0)
    settle(1, misc_text)
    store_image(unit_a(0, 0), finish(first_a))
    a_x = spread("x", unit_a(0, 0))
    a_y = {0: spread("y", unit_a(0, 0))}
    a_far, b_far = {}, {}
    scatter_second(first_b)
    captions_start(0, finish(first_t0))
    first_t1 = scatter_first(1, HALF, HALF, QUART)
    store_image(unit_b(0, 0), finish(first_b))
    b_y = spread("y", unit_b(0, 0))
    b_x = {0: spread("x", unit_b(0, 0))}
    a_x_far = pass_on("x", a_x, unit_a(-1, 0), unit_a(1, 0))
    for s in (-1, 1):
        a_y[s] = spread("y", unit_a(s, 0))
    scatter_second(first_t1)
    captions_step(0, 1)
    a_far[0] = pass_on("y", a_y[0], unit_a(0, -1), unit_a(0, 1))
    b_y_far = pass_on("y", b_y, unit_b(0, -1), unit_b(0, 1))
    for s in (-1, 1):
        b_x[s] = spread("x", unit_b(0, s))
    land(a_x_far, unit_a(2, 0))
    a_y[2] = spread("y", unit_a(2, 0))
    captions_start(1, finish(first_t1))
    land(b_y_far, unit_b(0, 2))
    b_x[2] = spread("x", unit_b(0, 2))
    b_far[0] = pass_on("x", b_x[0], unit_b(-1, 0), unit_b(1, 0))
    captions_step(0, 2)
    sibling(0)
    wave(0, 1, 0)
    captions_step(1, 1)
    for s in (-1, 1):
        a_far[s] = pass_on("y", a_y[s], unit_a(s, -1), unit_a(s, 1))
        b_far[s] = pass_on("x", b_x[s], unit_b(-1, s), unit_b(1, s))
    captions_step(0, 3)
    sibling(-1, 1)
    wave(0, 1, 1, 2)
    captions_step(1, 2)
    a_far[2] = pass_on("y", a_y[2], unit_a(2, -1), unit_a(2, 1))
    b_far[2] = pass_on("x", b_x[2], unit_b(-1, 2), unit_b(1, 2))
    captions_step(0, 4)
    wave(1, 2, 0, 1, 2)
    captions_step(1, 3)
    wave(2, 3, 0, 1, 2)
    sibling(-2, 2)
    wave(0, 3, 3, 4)
    captions_step(1, 4)
    for s in (0, -1, 1):
        land(a_far[s], unit_a(s, 2))
        land(b_far[s], unit_b(2, s))

    own_caps = txt[z, pl.ds(pl.multiple_of(core * PIECE, PIECE), PIECE), :]
    turn[...] = jnp.zeros_like(turn)
    turn[0:8, :] = pairs_ref[...].astype(F32)
    partner = turn[...].T
    mine = (piece * PIECE + lane).astype(F32)
    caption_positive = jnp.zeros((1, PIECE), F32)
    image_positive = jnp.zeros((PIECE, PIECE), F32)
    for p in range(8):
        t, px = p // 4, p % 4
        rows = jnp.concatenate(
            [
                img_a[yh * 2 + t, px * NA : (px + 1) * NA, :],
                img_b[px, pl.ds(pl.multiple_of((yh * 2 + t) * NB, 16), NB), :],
            ],
            axis=0,
        )
        scores = scale * lax.dot_general(
            rows, own_caps, (((1,), (1,)), ((), ())), preferred_element_type=F32
        )
        picked = jnp.where(partner[:, p : p + 1] == mine, scores, 0.0)
        caption_positive = caption_positive + jnp.sum(picked, axis=0, keepdims=True)
        image_positive = jnp.where(lane == p, jnp.sum(picked, axis=1, keepdims=True), image_positive)
    image_positive = image_positive.T

    sibling(-3, 3, 4)
    wave(0, 3, 5, 6, 7)
    land(a_far[2], unit_a(2, 2))
    land(b_far[2], unit_b(2, 2))
    wave(3, 4, 0, 1, 2, 3, 4, 5, 6, 7)

    for u in range(8):
        logs = (cmax[u] + jnp.log2(csum[u])) * LN2
        csend[2 * u] = logs[:, 0:PIECE]
        csend[2 * u + 1] = logs[:, PIECE : 2 * PIECE]
    me_column = z * 2 + core
    column_keys = []
    for where in column:
        target = wrap(z + where[2], 8) * 2 + lax.rem(core + where[3], 2)
        column_keys.append(send(csend.at[target], crecv.at[me_column], where))

    def flat_logs(max_ref, sum_ref, size):
        wide = lax.broadcasted_iota(jnp.int32, (size, PIECE), 1)
        logs = jnp.zeros((size, PIECE), F32)
        for u in range(4):
            logs = jnp.where(wide == u, (max_ref[u] + jnp.log2(sum_ref[u])) * LN2, logs)
        padded = -(-size // PIECE) * PIECE
        if padded > size:
            logs = jnp.concatenate([logs, jnp.zeros((padded - size, PIECE), F32)], axis=0)
        return jnp.concatenate([logs[i : i + PIECE].T for i in range(0, padded, PIECE)], axis=1)

    flat_a = flat_logs(rmax_a, rsum_a, 4 * NA)
    flat_b = flat_logs(rmax_b, rsum_b, 4 * NB)
    same = [(yh == 0).astype(F32), (yh == 1).astype(F32)]
    for py in range(4):
        for px in range(4):
            rsend[py * 4 + px, 0:1, :] = jnp.concatenate(
                [flat_a[py : py + 1, px * NA : (px + 1) * NA], flat_b[px : px + 1, py * NB : (py + 1) * NB]], axis=1
            )
            p = (py % 2) * 4 + px
            rsend[py * 4 + px, 1:2, :] = image_positive[p : p + 1, :] * same[py // 2]
    me_plane = y * 4 + x
    plane_keys = []
    for where in plane:
        target = wrap(y + where[1], 4) * 4 + wrap(x + where[0], 4)
        plane_keys.append(send(rsend.at[target], rrecv.at[me_plane], where))
    crecv[me_column] = csend[me_column]
    rrecv[me_plane] = rsend[me_plane]
    for where, k in zip(column, column_keys):
        source = wrap(z - where[2], 8) * 2 + lax.rem(core + where[3], 2)
        arrive(k, crecv.at[source])
    for where, k in zip(plane, plane_keys):
        source = wrap(y - where[1], 4) * 4 + wrap(x - where[0], 4)
        arrive(k, rrecv.at[source])

    def merge(rows):
        top = jnp.max(rows, axis=0)
        return top + jnp.log(jnp.sum(jnp.exp(rows - top[None]), axis=0))

    image_rows = rrecv[...]
    fsend[0:1, :] = merge(image_rows[:, 0:1, :]) - jnp.sum(image_rows[:, 1:2, :], axis=0)
    fsend[1:2, :] = merge(crecv[...]) - caption_positive
    shard = [(dx, dt) for dt in range(2) for dx in range(4) if (dx, dt) != (0, 0)]
    shard_keys = []
    step_y = [0, 1 - 2 * tw]
    for dx, dt in shard:
        shard_keys.append(send(fsend, frecv.at[piece], (dx, step_y[dt], 0, 0)))
    frecv[piece] = fsend[...]
    for (dx, dt), k in zip(shard, shard_keys):
        source = lax.rem(tw + dt, 2) * 4 + wrap(x - dx, 4)
        arrive(k, frecv.at[source])
    for p in range(8):
        out[p : p + 1, :] = frecv[p, 0:1, :]
        out[8 + p : 9 + p, :] = frecv[p, 1:2, :]
    for copy in sent:
        copy.wait_send()


def on_device(image_feats, text_feats, image_proj, text_proj, logit_scale, pairs):
    vmem = pl.BlockSpec(memory_space=pltpu.VMEM)
    hbm = pl.BlockSpec(memory_space=pl.ANY)
    losses = pl.pallas_call(
        kernel,
        out_shape=jax.ShapeDtypeStruct((16, 128), F32),
        in_specs=[hbm, hbm, hbm, hbm, pl.BlockSpec(memory_space=pltpu.SMEM), vmem],
        out_specs=vmem,
        scratch_shapes=[
            pltpu.VMEM((512, LOCAL[0]), BF16),
            pltpu.VMEM((LOCAL[1], 512), BF16),
            pltpu.VMEM((LOCAL[0], EMB), BF16),
            pltpu.VMEM((LOCAL[1], EMB), BF16),
            pltpu.VMEM((2, 512, 1), F32),
            pltpu.VMEM((2, 512, EMB), F32),
            pltpu.VMEM((2, 512, EMB), BF16),
            pltpu.VMEM((2, 4, 1, EMB + 256), F32),
            pltpu.VMEM((2, 4, 1, EMB + 256), F32),
            pltpu.VMEM((2, 2, PIECE, EMB), BF16),
            pltpu.VMEM((2, PIECE, EMB), BF16),
            pltpu.VMEM((2, 2, PIECE, EMB), BF16),
            pltpu.VMEM((PIECE, PIECE), F32),
            pltpu.VMEM((2, PIECE, PIECE), F32),
            pltpu.VMEM((4, 4 * NA, EMB), BF16),
            pltpu.VMEM((4, 4 * NB, EMB), BF16),
            pltpu.VMEM((8, 256, EMB), BF16),
            pltpu.VMEM((4, 4 * NA, 1), F32),
            pltpu.VMEM((4, 4 * NA, 1), F32),
            pltpu.VMEM((4, 4 * NB, 1), F32),
            pltpu.VMEM((4, 4 * NB, 1), F32),
            pltpu.VMEM((8, 1, 256), F32),
            pltpu.VMEM((8, 1, 256), F32),
            pltpu.VMEM((16, 2, PIECE), F32),
            pltpu.VMEM((16, 2, PIECE), F32),
            pltpu.VMEM((16, 1, PIECE), F32),
            pltpu.VMEM((16, 1, PIECE), F32),
            pltpu.VMEM((2, PIECE), F32),
            pltpu.VMEM((8, 2, PIECE), F32),
            pltpu.SemaphoreType.DMA((4,)),
            pltpu.SemaphoreType.DMA((NSEM,)),
            pltpu.SemaphoreType.DMA((NSEM,)),
        ],
        compiler_params=pltpu.CompilerParams(
            collective_id=0, has_side_effects=True, vmem_limit_bytes=60 * 1024 * 1024
        ),
    )(
        image_feats, text_feats.T, image_proj, text_proj,
        logit_scale.reshape(1, 1), pairs.reshape(8, 128),
    )
    return (losses[0:8].reshape(ROWS), losses[8:16].reshape(ROWS))


def solution(mesh):
    return jax.shard_map(
        on_device,
        mesh=mesh,
        in_specs=(
            P("blk", "mp"),
            P("blk", "mp"),
            P("mp", None),
            P("mp", None),
            P(),
            P("blk", None),
        ),
        out_specs=(P("blk"), P("blk")),
        check_vma=False,
    )
```

time: 99.8 us -> 87.1 us (0.87)
  Pallas kernels: 93.4 us -> 84.3 us
  local copies, waits for them, and re-layouts: 4.78 us -> 1.28 us
    pallas_call x1, Pallas kernels: 93.4 us -> 84.3 us  [on_device(): pl.pallas_call(kernel, out_shape=jax.ShapeDtypeStruct((16, 128), F32), in...]
    unnamed x3 -> x0, local copies, waits for them, and re-layouts: 4.78 us -> none
    reshape x0 -> x1, local copies, waits for them, and re-layouts: none -> 1.28 us  [on_device(): return (losses[0:8].reshape(ROWS), losses[8:16].reshape(ROWS))]
where the time goes in v2:
time: 87.1 us; the launch traced here: 86.9 us
  Pallas kernels  84.3 us (97%)
  between operations  1.29 us (1%)
  local copies, waits for them, and re-layouts  1.28 us (1%)
    pallas_call x1, Pallas kernels, on_device(): pl.pallas_call(kernel, out_shape=jax.ShapeDtypeStruct((16, 128), F32), in...  84.3 us

profile of v2, /device:TPU:8, one launch (start us, length us, event | category | flops | bytes accessed | tf_op | source)
XLA Modules:
  0.0 86.9 jit_solution(2854118073769384641)
XLA Ops:
  1.3 84.3 %shard_map.77 = f32[16,128]{1,0:T(8,128)} custom-call(bf16[1024,1280]{1,0:T(8,128)(2,1)} %imf.1, bf16[320,1024]{1,0:T(8,128)(2,1)} %bitcast.8, bf16[1280,1024]{1,0:T(8,128)(2,1)} %wim.1, bf16[320,1024]{1,0:T(8,128)(2,1)} %wtx.1, f32[1,1]{1,0:T(1,128)} %bitcast.7.scale_ref, s32[8,128]{1,0:T(8,128)} %bitcast.9), custom_call_target="tpu_custom_call" | custom-call | tf_op jit(solution)/shard_map/pallas_call | solution.py:469
  85.6 1.3 %slice_bitcast_fusion = (f32[1024]{0:T(1024)}, f32[1024]{0:T(1024)}) fusion(f32[16,128]{1,0:T(8,128)} %shard_map.77), kind=kLoop, calls=%fused_computation | loop fusion | bytes 16384 | tf_op jit(solution)/shard_map/reshape | solution.py:515

commit v3 on v2

--- a/solution.py
+++ b/solution.py
@@ -16,8 +16,115 @@
 HALF = 64
 QUART = 32
 NSEM = 160
-NA, NB = 80, 48
-CUT_A, CUT_B = 48, 16
+NA, NB = 64, 64
+CUT_A, CUT_B = 32, 32
+IMAGE_A, IMAGE_B, TEXT_0, TEXT_1 = range(4)
+KIND_A, KIND_B = 0, 1
+(
+    FIRST, FROM_LEFT, FROM_RIGHT, FINISH, STAGE_LOW, STAGE_HIGH, STAGE_FAR, PASS_LOW, PASS_HIGH, LAND,
+    CAPTION_LOW, CAPTION_HIGH, CAPTION_FAR, SIBLING, TILE, POSITIVE,
+) = range(16)
+ORDER = [
+    (FIRST, IMAGE_A),
+    (FIRST, TEXT_0),
+    (FIRST, IMAGE_B),
+    (FIRST, TEXT_1),
+    (FROM_RIGHT, IMAGE_A),
+    (FROM_LEFT, IMAGE_A),
+    (FROM_RIGHT, TEXT_0),
+    (FROM_LEFT, TEXT_0),
+    (FROM_LEFT, IMAGE_B),
+    (FROM_RIGHT, IMAGE_B),
+    (FROM_RIGHT, TEXT_1),
+    (FROM_LEFT, TEXT_1),
+    (FINISH, IMAGE_A),
+    (FINISH, TEXT_0),
+    (FINISH, IMAGE_B),
+    (SIBLING, 0, 0),
+    (FINISH, TEXT_1),
+    (SIBLING, 1, 0),
+    (PASS_LOW, KIND_A, 0),
+    (STAGE_LOW, KIND_A),
+    (CAPTION_LOW, 0, 1),
+    (STAGE_HIGH, KIND_A),
+    (CAPTION_HIGH, 0, 1),
+    (SIBLING, 0, 1),
+    (STAGE_LOW, KIND_B),
+    (STAGE_HIGH, KIND_B),
+    (CAPTION_HIGH, 1, 1),
+    (PASS_LOW, KIND_B, 0),
+    (CAPTION_LOW, 1, 1),
+    (STAGE_FAR, KIND_A),
+    (TILE, KIND_A, 0, (0,)),
+    (CAPTION_LOW, 0, 2),
+    (CAPTION_HIGH, 0, 2),
+    (SIBLING, 0, -2),
+    (PASS_LOW, KIND_B, -1),
+    (PASS_HIGH, KIND_B, -1),
+    (SIBLING, 1, -1),
+    (SIBLING, 1, 1),
+    (SIBLING, 0, -1),
+    (PASS_HIGH, KIND_A, 0),
+    (PASS_HIGH, KIND_B, 0),
+    (SIBLING, 0, 2),
+    (TILE, KIND_A, 0, (-1, 1)),
+    (PASS_HIGH, KIND_A, 1),
+    (CAPTION_LOW, 1, 2),
+    (CAPTION_HIGH, 1, 2),
+    (PASS_LOW, KIND_A, 1),
+    (STAGE_FAR, KIND_B),
+    (PASS_LOW, KIND_B, 1),
+    (SIBLING, 1, 2),
+    (PASS_HIGH, KIND_A, -1),
+    (SIBLING, 1, -2),
+    (PASS_LOW, KIND_A, -1),
+    (PASS_HIGH, KIND_B, 1),
+    (TILE, KIND_B, 0, (0, -1, 1, -2)),
+    (TILE, KIND_A, 0, (-2, 2)),
+    (CAPTION_HIGH, 0, 3),
+    (TILE, KIND_B, 0, (2,)),
+    (PASS_HIGH, KIND_A, 2),
+    (CAPTION_LOW, 0, 3),
+    (TILE, KIND_A, 1, (0, -1, 1, -2)),
+    (PASS_LOW, KIND_A, 2),
+    (TILE, KIND_A, -1, (0, -1, 1, -2)),
+    (TILE, KIND_A, -1, (2,)),
+    (TILE, KIND_A, 1, (2,)),
+    (LAND, KIND_A, 1),
+    (CAPTION_LOW, 1, 3),
+    (LAND, KIND_B, -1),
+    (CAPTION_HIGH, 1, 3),
+    (PASS_LOW, KIND_B, 2),
+    (LAND, KIND_A, 0),
+    (PASS_HIGH, KIND_B, 2),
+    (TILE, KIND_B, -1, (0, -1, 1, -2)),
+    (CAPTION_FAR, 0),
+    (SIBLING, 1, -3),
+    (SIBLING, 0, -3),
+    (SIBLING, 1, 3),
+    (TILE, KIND_B, 1, (0, -1, 1, -2)),
+    (TILE, KIND_B, -1, (2, -3)),
+    (LAND, KIND_A, 2),
+    (LAND, KIND_B, 1),
+    (LAND, KIND_A, -1),
+    (SIBLING, 0, 3),
+    (LAND, KIND_B, 0),
+    (POSITIVE,),
+    (TILE, KIND_A, 2, (0, -1, 1, -2)),
+    (LAND, KIND_B, 2),
+    (SIBLING, 0, 4),
+    (CAPTION_FAR, 1),
+    (TILE, KIND_B, 2, (0, -1, 1, -2)),
+    (SIBLING, 1, 4),
+    (TILE, KIND_A, 2, (2, -3, 3, 4)),
+    (TILE, KIND_B, 1, (2, -3, 3, 4)),
+    (TILE, KIND_B, 2, (2, -3, 3, 4)),
+    (TILE, KIND_A, 0, (-3, 3, 4)),
+    (TILE, KIND_A, -1, (-3, 3, 4)),
+    (TILE, KIND_A, 1, (-3, 3, 4)),
+    (TILE, KIND_B, 0, (-3, 3, 4)),
+    (TILE, KIND_B, -1, (3, 4)),
+]
 LOG2E = 1.4426950408889634
 LN2 = 0.6931471805599453
 LOW = -1e30
@@ -29,7 +136,7 @@
 
 def kernel(
     imf, txf, wim, wtx, scale_ref, pairs_ref, out,
-    xi, xt, wi, wt, mus, pf, pb, misc_send, misc_recv, relay, comb, fin, turn, columns,
+    xi, xt, xtt, wi, wt, mus, pf, pb, misc_send, misc_recv, relay, comb, fin, turn, columns,
     img_a, img_b, txt, rmax_a, rsum_a, rmax_b, rsum_b, cmax, csum,
     rsend, rrecv, csend, crecv, fsend, frecv, lsem, ssem, rsem,
 ):
@@ -80,8 +187,8 @@
     plane = [(dx, dy, 0, 0) for dy in range(4) for dx in range(4) if (dx, dy) != (0, 0)]
     column = [(0, 0, dz, dc) for dz in range(8) for dc in range(2) if (dz, dc) != (0, 0)]
     barrier = pltpu.get_barrier_semaphore()
-    for where in plane + column:
-        pl.semaphore_signal(barrier, inc=1, device_id=device(*where), device_id_type=MESH)
+    for to in plane + column:
+        pl.semaphore_signal(barrier, inc=1, device_id=device(*to), device_id_type=MESH)
 
     lane = lax.broadcasted_iota(jnp.int32, (PIECE, PIECE), 1)
 
@@ -108,13 +215,16 @@
             return carry
 
         lax.fori_loop(0, 4, rows_stats, 0)
-        contract = (((1,), (0,)), ((), ())) if q == 0 else (((0,), (0,)), ((), ()))
+        lhs = feats
+        if q == 1:
+            lhs = xtt
+            lhs[...] = feats[...].T
 
         def columns_step(n, carry):
             cols = pl.ds(pl.multiple_of(n * 256, 256), 256)
             block = weights[:, cols]
             total = jnp.dot(jnp.ones((8, width), BF16), block, preferred_element_type=F32)[0:1, :]
-            part = lax.dot_general(feats[...], block, contract, preferred_element_type=F32) - mus[q] * total
+            part = jnp.dot(lhs[...], block, preferred_element_type=F32) - mus[q] * total
             pf[q, :, cols] = part
             pb[q, :, cols] = part.astype(BF16)
             for d in range(4):
@@ -145,18 +255,6 @@
             "fin1a": send(pb.at[q, part_rows(left, start, cut), :], fin.at[q, 1, low, :], (3, 0, 0, 0)),
         }
 
-    def scatter_second(keys):
-        q, start, count, cut = keys["batch"]
-        low, high = pl.ds(start, cut), pl.ds(start + cut, count - cut)
-        arrive(keys["relay0"], relay.at[q, 0, low, :])
-        comb[q, low, :] = (pf[q, part_rows(right, start, cut), :] + relay[q, 0, low, :].astype(F32)).astype(BF16)
-        keys["fin0a"] = send(comb.at[q, low, :], fin.at[q, 0, low, :], (1, 0, 0, 0))
-        arrive(keys["relay1"], relay.at[q, 1, high, :])
-        comb[q, high, :] = (
-            pf[q, part_rows(left, start + cut, count - cut), :] + relay[q, 1, high, :].astype(F32)
-        ).astype(BF16)
-        keys["fin1b"] = send(comb.at[q, high, :], fin.at[q, 1, high, :], (3, 0, 0, 0))
-
     def settle(q, keys):
         for d, k in zip((1, 3, 2), keys):
             arrive(k, misc_recv.at[q, wrap(x - d, 4)])
@@ -204,17 +302,6 @@
         ref = chunk(where)
         return [send(ref, ref, move[axis](1)), send(ref, ref, move[axis](3))]
 
-    def pass_on(axis, keys, lower, upper):
-        arrive(keys[0], chunk(lower))
-        low = send(chunk(lower, 0), chunk(lower, 0), move[axis](1))
-        arrive(keys[1], chunk(upper))
-        high = send(chunk(upper, 1), chunk(upper, 1), move[axis](3))
-        return low, high
-
-    def land(keys, far):
-        arrive(keys[0], chunk(far, 0))
-        arrive(keys[1], chunk(far, 1))
-
     def store_image(where, rows):
         ref, size, unit, place = where
         ref[unit, pl.ds(pl.multiple_of(place * size, 16), size), :] = rows
@@ -223,45 +310,8 @@
         place = lax.rem(core + other, 2) * PIECE + half * HALF
         return txt.at[wrap(z + dz, 8), pl.ds(pl.multiple_of(place + start, 16), count), :]
 
-    up, down, pair_keys = {}, {}, {}
-
-    def captions_start(half, rows):
-        txt[z, pl.ds(pl.multiple_of(core * PIECE + half * HALF, HALF), HALF), :] = rows
-        up[half, 1] = send(cap(0, half), cap(0, half), (0, 0, 1, 0))
-        down[half, 1] = send(cap(0, half), cap(0, half), (0, 0, 7, 0))
-        pair_keys[half, 0] = send(cap(0, half), cap(0, half), (0, 0, 0, 1))
-
-    def captions_step(half, d):
-        if d < 4:
-            arrive(up[half, d], cap(-d, half))
-            if d < 3:
-                up[half, d + 1] = send(cap(-d, half), cap(-d, half), (0, 0, 1, 0))
-            else:
-                up[half, 4] = send(cap(-3, half, 0, 0, QUART), cap(-3, half, 0, 0, QUART), (0, 0, 1, 0))
-            arrive(down[half, d], cap(d, half))
-            if d < 3:
-                down[half, d + 1] = send(cap(d, half), cap(d, half), (0, 0, 7, 0))
-            else:
-                down[half, 4] = send(cap(3, half, 0, QUART, QUART), cap(3, half, 0, QUART, QUART), (0, 0, 7, 0))
-            pair_keys[half, -d] = send(cap(-d, half), cap(-d, half), (0, 0, 0, 1))
-            pair_keys[half, d] = send(cap(d, half), cap(d, half), (0, 0, 0, 1))
-        else:
-            arrive(up[half, 4], cap(4, half, 0, 0, QUART))
-            arrive(down[half, 4], cap(4, half, 0, QUART, QUART))
-            pair_keys[half, 4] = send(cap(4, half), cap(4, half), (0, 0, 0, 1))
-
-    def sibling(*offsets):
-        for dz in offsets:
-            for half in (0, 1):
-                arrive(pair_keys[half, dz], cap(dz, half, 1))
-
     scale = scale_ref[0, 0]
     scale2 = scale * LOG2E
-
-    def signed(k):
-        if isinstance(k, int):
-            return ((k + 1) // 2) * (1 - 2 * ((k + 1) % 2))
-        return ((k + 1) // 2) * (1 - 2 * lax.rem(k + 1, 2))
 
     def update(max_ref, sum_ref, unit, top, total):
         old, held = max_ref[unit], sum_ref[unit]
@@ -271,8 +321,8 @@
         max_ref[unit] = jnp.maximum(old, top)
         sum_ref[unit] = jnp.where(keep, held, total) + jnp.where(keep, total, held) * small
 
-    def group(images, max_ref, sum_ref, unit, ks):
-        units = [wrap(z + signed(k), 8) for k in ks]
+    def group(images, max_ref, sum_ref, unit, offsets):
+        units = [wrap(z + dz, 8) for dz in offsets]
         scores = [
             scale2 * lax.dot_general(images[unit], txt[v], (((1,), (1,)), ((), ())), preferred_element_type=F32)
             for v in units
@@ -289,112 +339,201 @@
             total = total + jnp.exp2(block - top)
         update(max_ref, sum_ref, unit, top, jnp.sum(total, axis=1, keepdims=True))
 
-    def wave(j0, j1, *ks):
-        def step(j, carry):
-            group(img_a, rmax_a, rsum_a, wrap(y + signed(j), 4), ks)
-            group(img_b, rmax_b, rsum_b, wrap(x + signed(j), 4), ks)
-            return carry
-
-        lax.fori_loop(j0, j1, step, 0)
+    tasks = {}
+    BATCH = {
+        IMAGE_A: (0, 0, NA, CUT_A),
+        IMAGE_B: (0, NA, NB, CUT_B),
+        TEXT_0: (1, 0, HALF, QUART),
+        TEXT_1: (1, HALF, HALF, QUART),
+    }
+
+    def start_batch(name):
+        q, start, count, cut = BATCH[name]
+        low, high = pl.ds(start, cut), pl.ds(start + cut, count - cut)
+        keys = scatter_first(q, start, count, cut)
+
+        def from_left():
+            arrive(keys["relay0"], relay.at[q, 0, low, :])
+            comb[q, low, :] = (
+                pf[q, part_rows(right, start, cut), :] + relay[q, 0, low, :].astype(F32)
+            ).astype(BF16)
+            keys["fin0a"] = send(comb.at[q, low, :], fin.at[q, 0, low, :], (1, 0, 0, 0))
+
+        def from_right():
+            arrive(keys["relay1"], relay.at[q, 1, high, :])
+            comb[q, high, :] = (
+                pf[q, part_rows(left, start + cut, count - cut), :] + relay[q, 1, high, :].astype(F32)
+            ).astype(BF16)
+            keys["fin1b"] = send(comb.at[q, high, :], fin.at[q, 1, high, :], (3, 0, 0, 0))
+
+        def last():
+            if name in (IMAGE_A, TEXT_0):
+                settle(q, misc_keys[q])
+            rows = finish(keys)
+            if name == IMAGE_A:
+                store_image(unit_a(0, 0), rows)
+                stage("x", KIND_A, spread("x", unit_a(0, 0)))
+                second_stage("y", KIND_A, 0, spread("y", unit_a(0, 0)))
+            elif name == IMAGE_B:
+                store_image(unit_b(0, 0), rows)
+                stage("y", KIND_B, spread("y", unit_b(0, 0)))
+                second_stage("x", KIND_B, 0, spread("x", unit_b(0, 0)))
+            else:
+                half = name - TEXT_0
+                txt[z, pl.ds(pl.multiple_of(core * PIECE + half * HALF, HALF), HALF), :] = rows
+                ref = cap(0, half)
+                low_key, high_key = send(ref, ref, (0, 0, 1, 0)), send(ref, ref, (0, 0, 7, 0))
+                to_sibling(half, 0)
+                captions(half, 1, low_key, high_key)
+
+        tasks[FROM_LEFT, name] = from_left
+        tasks[FROM_RIGHT, name] = from_right
+        tasks[FINISH, name] = last
+
+    def where(kind, along, across):
+        return unit_a(along, across) if kind == KIND_A else unit_b(across, along)
+
+    def stage(axis, kind, keys):
+        other = "y" if axis == "x" else "x"
+        far = {}
+
+        def lower():
+            ref = where(kind, -1, 0)
+            arrive(keys[0], chunk(ref))
+            far[0] = send(chunk(ref, 0), chunk(ref, 0), move[axis](1))
+            second_stage(other, kind, -1, spread(other, ref))
+
+        def upper():
+            ref = where(kind, 1, 0)
+            arrive(keys[1], chunk(ref))
+            far[1] = send(chunk(ref, 1), chunk(ref, 1), move[axis](3))
+            second_stage(other, kind, 1, spread(other, ref))
+
+        def opposite_chunk():
+            ref = where(kind, 2, 0)
+            arrive(far[0], chunk(ref, 0))
+            arrive(far[1], chunk(ref, 1))
+            second_stage(other, kind, 2, spread(other, ref))
+
+        tasks[STAGE_LOW, kind] = lower
+        tasks[STAGE_HIGH, kind] = upper
+        tasks[STAGE_FAR, kind] = opposite_chunk
+
+    def second_stage(axis, kind, s, keys):
+        far = {}
+
+        def lower():
+            ref = where(kind, s, -1)
+            arrive(keys[0], chunk(ref))
+            far[0] = send(chunk(ref, 0), chunk(ref, 0), move[axis](1))
+
+        def upper():
+            ref = where(kind, s, 1)
+            arrive(keys[1], chunk(ref))
+            far[1] = send(chunk(ref, 1), chunk(ref, 1), move[axis](3))
+
+        def land():
+            ref = where(kind, s, 2)
+            arrive(far[0], chunk(ref, 0))
+            arrive(far[1], chunk(ref, 1))
+
+        tasks[PASS_LOW, kind, s] = lower
+        tasks[PASS_HIGH, kind, s] = upper
+        tasks[LAND, kind, s] = land
+
+    def to_sibling(half, dz):
+        key = send(cap(dz, half), cap(dz, half), (0, 0, 0, 1))
+        tasks[SIBLING, half, dz] = lambda: arrive(key, cap(dz, half, 1))
+
+    def captions(half, d, low_key, high_key):
+        keys = {}
+
+        def follow():
+            if len(keys) < 2:
+                return
+            if d < 3:
+                captions(half, d + 1, keys[0], keys[1])
+                return
+
+            def opposite_caption():
+                arrive(keys[0], cap(4, half, 0, 0, QUART))
+                arrive(keys[1], cap(4, half, 0, QUART, QUART))
+                to_sibling(half, 4)
+
+            tasks[CAPTION_FAR, half] = opposite_caption
+
+        def lower():
+            arrive(low_key, cap(-d, half))
+            ref = cap(-d, half) if d < 3 else cap(-d, half, 0, 0, QUART)
+            keys[0] = send(ref, ref, (0, 0, 1, 0))
+            to_sibling(half, -d)
+            follow()
+
+        def upper():
+            arrive(high_key, cap(d, half))
+            ref = cap(d, half) if d < 3 else cap(d, half, 0, QUART, QUART)
+            keys[1] = send(ref, ref, (0, 0, 7, 0))
+            to_sibling(half, d)
+            follow()
+
+        tasks[CAPTION_LOW, half, d] = lower
+        tasks[CAPTION_HIGH, half, d] = upper
+
+    def positives():
+        own_caps = txt[z, pl.ds(pl.multiple_of(core * PIECE, PIECE), PIECE), :]
+        turn[...] = jnp.zeros_like(turn)
+        turn[0:8, :] = pairs_ref[...].astype(F32)
+        partner = turn[...].T
+        mine = (piece * PIECE + lane).astype(F32)
+        caption_positive = jnp.zeros((1, PIECE), F32)
+        image_positive = jnp.zeros((PIECE, PIECE), F32)
+        for p in range(8):
+            t, px = p // 4, p % 4
+            rows = jnp.concatenate(
+                [
+                    img_a[yh * 2 + t, px * NA : (px + 1) * NA, :],
+                    img_b[px, pl.ds(pl.multiple_of((yh * 2 + t) * NB, 16), NB), :],
+                ],
+                axis=0,
+            )
+            scores = scale * lax.dot_general(
+                rows, own_caps, (((1,), (1,)), ((), ())), preferred_element_type=F32
+            )
+            picked = jnp.where(partner[:, p : p + 1] == mine, scores, 0.0)
+            caption_positive = caption_positive + jnp.sum(picked, axis=0, keepdims=True)
+            image_positive = jnp.where(lane == p, jnp.sum(picked, axis=1, keepdims=True), image_positive)
+        image_positive = image_positive.T
+
+        return caption_positive, image_positive
 
     loads[0].wait()
     loads[1].wait()
     project(0, xi, wi)
     pl.semaphore_wait(barrier, len(plane) + len(column))
-    first_a = scatter_first(0, 0, NA, CUT_A)
-    misc_image = scatter_misc(0)
-    loads[2].wait()
-    loads[3].wait()
-    project(1, xt, wt)
-    first_t0 = scatter_first(1, 0, HALF, QUART)
-    misc_text = scatter_misc(1)
-    for ref in (rmax_a, rmax_b, cmax):
-        ref[...] = jnp.full(ref.shape, LOW, F32)
-    for ref in (rsum_a, rsum_b, csum):
-        ref[...] = jnp.zeros(ref.shape, F32)
-    scatter_second(first_a)
-    settle(0, misc_image)
-    first_b = scatter_first(0, NA, NB, CUT_B)
-    scatter_second(first_t0)
-    settle(1, misc_text)
-    store_image(unit_a(0, 0), finish(first_a))
-    a_x = spread("x", unit_a(0, 0))
-    a_y = {0: spread("y", unit_a(0, 0))}
-    a_far, b_far = {}, {}
-    scatter_second(first_b)
-    captions_start(0, finish(first_t0))
-    first_t1 = scatter_first(1, HALF, HALF, QUART)
-    store_image(unit_b(0, 0), finish(first_b))
-    b_y = spread("y", unit_b(0, 0))
-    b_x = {0: spread("x", unit_b(0, 0))}
-    a_x_far = pass_on("x", a_x, unit_a(-1, 0), unit_a(1, 0))
-    for s in (-1, 1):
-        a_y[s] = spread("y", unit_a(s, 0))
-    scatter_second(first_t1)
-    captions_step(0, 1)
-    a_far[0] = pass_on("y", a_y[0], unit_a(0, -1), unit_a(0, 1))
-    b_y_far = pass_on("y", b_y, unit_b(0, -1), unit_b(0, 1))
-    for s in (-1, 1):
-        b_x[s] = spread("x", unit_b(0, s))
-    land(a_x_far, unit_a(2, 0))
-    a_y[2] = spread("y", unit_a(2, 0))
-    captions_start(1, finish(first_t1))
-    land(b_y_far, unit_b(0, 2))
-    b_x[2] = spread("x", unit_b(0, 2))
-    b_far[0] = pass_on("x", b_x[0], unit_b(-1, 0), unit_b(1, 0))
-    captions_step(0, 2)
-    sibling(0)
-    wave(0, 1, 0)
-    captions_step(1, 1)
-    for s in (-1, 1):
-        a_far[s] = pass_on("y", a_y[s], unit_a(s, -1), unit_a(s, 1))
-        b_far[s] = pass_on("x", b_x[s], unit_b(-1, s), unit_b(1, s))
-    captions_step(0, 3)
-    sibling(-1, 1)
-    wave(0, 1, 1, 2)
-    captions_step(1, 2)
-    a_far[2] = pass_on("y", a_y[2], unit_a(2, -1), unit_a(2, 1))
-    b_far[2] = pass_on("x", b_x[2], unit_b(-1, 2), unit_b(1, 2))
-    captions_step(0, 4)
-    wave(1, 2, 0, 1, 2)
-    captions_step(1, 3)
-    wave(2, 3, 0, 1, 2)
-    sibling(-2, 2)
-    wave(0, 3, 3, 4)
-    captions_step(1, 4)
-    for s in (0, -1, 1):
-        land(a_far[s], unit_a(s, 2))
-        land(b_far[s], unit_b(2, s))
-
-    own_caps = txt[z, pl.ds(pl.multiple_of(core * PIECE, PIECE), PIECE), :]
-    turn[...] = jnp.zeros_like(turn)
-    turn[0:8, :] = pairs_ref[...].astype(F32)
-    partner = turn[...].T
-    mine = (piece * PIECE + lane).astype(F32)
-    caption_positive = jnp.zeros((1, PIECE), F32)
-    image_positive = jnp.zeros((PIECE, PIECE), F32)
-    for p in range(8):
-        t, px = p // 4, p % 4
-        rows = jnp.concatenate(
-            [
-                img_a[yh * 2 + t, px * NA : (px + 1) * NA, :],
-                img_b[px, pl.ds(pl.multiple_of((yh * 2 + t) * NB, 16), NB), :],
-            ],
-            axis=0,
-        )
-        scores = scale * lax.dot_general(
-            rows, own_caps, (((1,), (1,)), ((), ())), preferred_element_type=F32
-        )
-        picked = jnp.where(partner[:, p : p + 1] == mine, scores, 0.0)
-        caption_positive = caption_positive + jnp.sum(picked, axis=0, keepdims=True)
-        image_positive = jnp.where(lane == p, jnp.sum(picked, axis=1, keepdims=True), image_positive)
-    image_positive = image_positive.T
-
-    sibling(-3, 3, 4)
-    wave(0, 3, 5, 6, 7)
-    land(a_far[2], unit_a(2, 2))
-    land(b_far[2], unit_b(2, 2))
-    wave(3, 4, 0, 1, 2, 3, 4, 5, 6, 7)
+    misc_keys = {}
+    for item in ORDER:
+        if item[0] == TILE:
+            _, kind, offset, offsets = item
+            if kind == KIND_A:
+                group(img_a, rmax_a, rsum_a, wrap(y + offset, 4), offsets)
+            else:
+                group(img_b, rmax_b, rsum_b, wrap(x + offset, 4), offsets)
+        elif item[0] == POSITIVE:
+            caption_positive, image_positive = positives()
+        elif item[0] == FIRST:
+            start_batch(item[1])
+            if item[1] == IMAGE_A:
+                misc_keys[0] = scatter_misc(0)
+                loads[2].wait()
+                loads[3].wait()
+                project(1, xt, wt)
+                misc_keys[1] = scatter_misc(1)
+                for ref in (rmax_a, rmax_b, cmax):
+                    ref[...] = jnp.full(ref.shape, LOW, F32)
+                for ref in (rsum_a, rsum_b, csum):
+                    ref[...] = jnp.zeros(ref.shape, F32)
+        else:
+            tasks.pop(item)()
 
     for u in range(8):
         logs = (cmax[u] + jnp.log2(csum[u])) * LN2
@@ -402,9 +541,9 @@
         csend[2 * u + 1] = logs[:, PIECE : 2 * PIECE]
     me_column = z * 2 + core
     column_keys = []
-    for where in column:
-        target = wrap(z + where[2], 8) * 2 + lax.rem(core + where[3], 2)
-        column_keys.append(send(csend.at[target], crecv.at[me_column], where))
+    for to in column:
+        target = wrap(z + to[2], 8) * 2 + lax.rem(core + to[3], 2)
+        column_keys.append(send(csend.at[target], crecv.at[me_column], to))
 
     def flat_logs(max_ref, sum_ref, size):
         wide = lax.broadcasted_iota(jnp.int32, (size, PIECE), 1)
@@ -428,16 +567,16 @@
             rsend[py * 4 + px, 1:2, :] = image_positive[p : p + 1, :] * same[py // 2]
     me_plane = y * 4 + x
     plane_keys = []
-    for where in plane:
-        target = wrap(y + where[1], 4) * 4 + wrap(x + where[0], 4)
-        plane_keys.append(send(rsend.at[target], rrecv.at[me_plane], where))
+    for to in plane:
+        target = wrap(y + to[1], 4) * 4 + wrap(x + to[0], 4)
+        plane_keys.append(send(rsend.at[target], rrecv.at[me_plane], to))
     crecv[me_column] = csend[me_column]
     rrecv[me_plane] = rsend[me_plane]
-    for where, k in zip(column, column_keys):
-        source = wrap(z - where[2], 8) * 2 + lax.rem(core + where[3], 2)
+    for to, k in zip(column, column_keys):
+        source = wrap(z - to[2], 8) * 2 + lax.rem(core + to[3], 2)
         arrive(k, crecv.at[source])
-    for where, k in zip(plane, plane_keys):
-        source = wrap(y - where[1], 4) * 4 + wrap(x - where[0], 4)
+    for to, k in zip(plane, plane_keys):
+        source = wrap(y - to[1], 4) * 4 + wrap(x - to[0], 4)
         arrive(k, rrecv.at[source])
 
     def merge(rows):
@@ -474,6 +613,7 @@
         scratch_shapes=[
             pltpu.VMEM((512, LOCAL[0]), BF16),
             pltpu.VMEM((LOCAL[1], 512), BF16),
+            pltpu.VMEM((512, LOCAL[1]), BF16),
             pltpu.VMEM((LOCAL[0], EMB), BF16),
             pltpu.VMEM((LOCAL[1], EMB), BF16),
             pltpu.VMEM((2, 512, 1), F32),

time: 87.1 us -> 77.1 us (0.89)
  Pallas kernels: 84.3 us -> 74.3 us
    pallas_call x1, Pallas kernels: 84.3 us -> 74.3 us  [on_device(): pl.pallas_call(kernel, out_shape=jax.ShapeDtypeStruct((16, 128), F32), in...]
where the time goes in v3:
time: 77.1 us; the launch traced here: 76.9 us
  Pallas kernels  74.3 us (96%)
  between operations  1.29 us (2%)
  local copies, waits for them, and re-layouts  1.28 us (2%)
    pallas_call x1, Pallas kernels, on_device(): pl.pallas_call(kernel, out_shape=jax.ShapeDtypeStruct((16, 128), F32), in...  74.3 us

profile of v3, /device:TPU:8, one launch (start us, length us, event | category | flops | bytes accessed | tf_op | source)
XLA Modules:
  0.0 76.9 jit_solution(9206274656321132025)
XLA Ops:
  1.3 74.3 %shard_map.77 = f32[16,128]{1,0:T(8,128)} custom-call(bf16[1024,1280]{1,0:T(8,128)(2,1)} %imf.1, bf16[320,1024]{1,0:T(8,128)(2,1)} %bitcast.8, bf16[1280,1024]{1,0:T(8,128)(2,1)} %wim.1, bf16[320,1024]{1,0:T(8,128)(2,1)} %wtx.1, f32[1,1]{1,0:T(1,128)} %bitcast.7.scale_ref, s32[8,128]{1,0:T(8,128)} %bitcast.9), custom_call_target="tpu_custom_call" | custom-call | tf_op jit(solution)/shard_map/pallas_call | solution.py:608
  75.6 1.3 %slice_bitcast_fusion = (f32[1024]{0:T(1024)}, f32[1024]{0:T(1024)}) fusion(f32[16,128]{1,0:T(8,128)} %shard_map.77), kind=kLoop, calls=%fused_computation | loop fusion | bytes 16384 | tf_op jit(solution)/shard_map/reshape | solution.py:655

commit v4 on v3

--- a/solution.py
+++ b/solution.py
@@ -20,6 +20,7 @@
 CUT_A, CUT_B = 32, 32
 IMAGE_A, IMAGE_B, TEXT_0, TEXT_1 = range(4)
 KIND_A, KIND_B = 0, 1
+MERGE = 2
 (
     FIRST, FROM_LEFT, FROM_RIGHT, FINISH, STAGE_LOW, STAGE_HIGH, STAGE_FAR, PASS_LOW, PASS_HIGH, LAND,
     CAPTION_LOW, CAPTION_HIGH, CAPTION_FAR, SIBLING, TILE, POSITIVE,
@@ -321,23 +322,44 @@
         max_ref[unit] = jnp.maximum(old, top)
         sum_ref[unit] = jnp.where(keep, held, total) + jnp.where(keep, total, held) * small
 
-    def group(images, max_ref, sum_ref, unit, offsets):
-        units = [wrap(z + dz, 8) for dz in offsets]
+    def group(members, offsets):
+        columns_of = [wrap(z + dz, 8) for dz in offsets]
         scores = [
-            scale2 * lax.dot_general(images[unit], txt[v], (((1,), (1,)), ((), ())), preferred_element_type=F32)
-            for v in units
+            [
+                scale2 * lax.dot_general(images[unit], txt[v], (((1,), (1,)), ((), ())), preferred_element_type=F32)
+                for v in columns_of
+            ]
+            for images, max_ref, sum_ref, unit in members
         ]
-        for v, block in zip(units, scores):
-            top = jnp.max(block, axis=0, keepdims=True)
-            update(cmax, csum, v, top, jnp.sum(jnp.exp2(block - top), axis=0, keepdims=True))
-        widest = scores[0]
-        for block in scores[1:]:
-            widest = jnp.maximum(widest, block)
-        top = jnp.max(widest, axis=1, keepdims=True)
-        total = jnp.exp2(scores[0] - top)
-        for block in scores[1:]:
-            total = total + jnp.exp2(block - top)
-        update(max_ref, sum_ref, unit, top, jnp.sum(total, axis=1, keepdims=True))
+        for i, v in enumerate(columns_of):
+            top = jnp.max(scores[0][i], axis=0, keepdims=True)
+            for row in scores[1:]:
+                top = jnp.maximum(top, jnp.max(row[i], axis=0, keepdims=True))
+            total = jnp.sum(jnp.exp2(scores[0][i] - top), axis=0, keepdims=True)
+            for row in scores[1:]:
+                total = total + jnp.sum(jnp.exp2(row[i] - top), axis=0, keepdims=True)
+            update(cmax, csum, v, top, total)
+        for row, (images, max_ref, sum_ref, unit) in zip(scores, members):
+            widest = row[0]
+            for block in row[1:]:
+                widest = jnp.maximum(widest, block)
+            top = jnp.max(widest, axis=1, keepdims=True)
+            total = jnp.exp2(row[0] - top)
+            for block in row[1:]:
+                total = total + jnp.exp2(block - top)
+            update(max_ref, sum_ref, unit, top, jnp.sum(total, axis=1, keepdims=True))
+
+    def tile_run(items):
+        merged = {}
+        for _, kind, offset, offsets in items:
+            if kind == KIND_A:
+                member = (img_a, rmax_a, rsum_a, wrap(y + offset, 4))
+            else:
+                member = (img_b, rmax_b, rsum_b, wrap(x + offset, 4))
+            merged.setdefault(offsets, []).append(member)
+        for offsets, members in merged.items():
+            for i in range(0, len(members), MERGE):
+                group(members[i : i + MERGE], offsets)
 
     tasks = {}
     BATCH = {
@@ -511,14 +533,16 @@
     project(0, xi, wi)
     pl.semaphore_wait(barrier, len(plane) + len(column))
     misc_keys = {}
-    for item in ORDER:
-        if item[0] == TILE:
-            _, kind, offset, offsets = item
-            if kind == KIND_A:
-                group(img_a, rmax_a, rsum_a, wrap(y + offset, 4), offsets)
-            else:
-                group(img_b, rmax_b, rsum_b, wrap(x + offset, 4), offsets)
-        elif item[0] == POSITIVE:
+    run = []
+    for item in ORDER + [None]:
+        if item is not None and item[0] == TILE:
+            run.append(item)
+            continue
+        tile_run(run)
+        run = []
+        if item is None:
+            break
+        if item[0] == POSITIVE:
             caption_positive, image_positive = positives()
         elif item[0] == FIRST:
             start_batch(item[1])
@@ -572,6 +596,9 @@
         plane_keys.append(send(rsend.at[target], rrecv.at[me_plane], to))
     crecv[me_column] = csend[me_column]
     rrecv[me_plane] = rsend[me_plane]
+    early = len(sent) - len(column) - len(plane)
+    for copy in sent[:early]:
+        copy.wait_send()
     for to, k in zip(column, column_keys):
         source = wrap(z - to[2], 8) * 2 + lax.rem(core + to[3], 2)
         arrive(k, crecv.at[source])
@@ -598,7 +625,7 @@
     for p in range(8):
         out[p : p + 1, :] = frecv[p, 0:1, :]
         out[8 + p : 9 + p, :] = frecv[p, 1:2, :]
-    for copy in sent:
+    for copy in sent[early:]:
         copy.wait_send()
 
 

time: 77.1 us -> 76.7 us (level)
  no operation moved by 1% of the time
where the time goes in v4:
time: 76.7 us; the launch traced here: 76.6 us
  Pallas kernels  74 us (96%)
  between operations  1.29 us (2%)
  local copies, waits for them, and re-layouts  1.28 us (2%)
    pallas_call x1, Pallas kernels, on_device(): pl.pallas_call(kernel, out_shape=jax.ShapeDtypeStruct((16, 128), F32), in...  74 us

profile of v4, /device:TPU:8, one launch (start us, length us, event | category | flops | bytes accessed | tf_op | source)
XLA Modules:
  0.0 76.6 jit_solution(16128321107002409074)
XLA Ops:
  1.3 74.0 %shard_map.77 = f32[16,128]{1,0:T(8,128)} custom-call(bf16[1024,1280]{1,0:T(8,128)(2,1)} %imf.1, bf16[320,1024]{1,0:T(8,128)(2,1)} %bitcast.8, bf16[1280,1024]{1,0:T(8,128)(2,1)} %wim.1, bf16[320,1024]{1,0:T(8,128)(2,1)} %wtx.1, f32[1,1]{1,0:T(1,128)} %bitcast.7.scale_ref, s32[8,128]{1,0:T(8,128)} %bitcast.9), custom_call_target="tpu_custom_call" | custom-call | tf_op jit(solution)/shard_map/pallas_call | solution.py:635
  75.3 1.3 %slice_bitcast_fusion = (f32[1024]{0:T(1024)}, f32[1024]{0:T(1024)}) fusion(f32[16,128]{1,0:T(8,128)} %shard_map.77), kind=kLoop, calls=%fused_computation | loop fusion | bytes 16384 | tf_op jit(solution)/shard_map/reshape | solution.py:682

commit v5 on v4

--- a/solution.py
+++ b/solution.py
@@ -20,7 +20,7 @@
 CUT_A, CUT_B = 32, 32
 IMAGE_A, IMAGE_B, TEXT_0, TEXT_1 = range(4)
 KIND_A, KIND_B = 0, 1
-MERGE = 2
+MERGE = 4
 (
     FIRST, FROM_LEFT, FROM_RIGHT, FINISH, STAGE_LOW, STAGE_HIGH, STAGE_FAR, PASS_LOW, PASS_HIGH, LAND,
     CAPTION_LOW, CAPTION_HIGH, CAPTION_FAR, SIBLING, TILE, POSITIVE,

time: 76.7 us -> 76.6 us (level)
  no operation moved by 1% of the time
where the time goes in v5:
time: 76.6 us; the launch traced here: 76.4 us
  Pallas kernels  73.9 us (96%)
  between operations  1.29 us (2%)
  local copies, waits for them, and re-layouts  1.28 us (2%)
    pallas_call x1, Pallas kernels, on_device(): pl.pallas_call(kernel, out_shape=jax.ShapeDtypeStruct((16, 128), F32), in...  73.9 us

profile of v5, /device:TPU:8, one launch (start us, length us, event | category | flops | bytes accessed | tf_op | source)
XLA Modules:
  0.0 76.4 jit_solution(3703411521115858511)
XLA Ops:
  1.3 73.9 %shard_map.77 = f32[16,128]{1,0:T(8,128)} custom-call(bf16[1024,1280]{1,0:T(8,128)(2,1)} %imf.1, bf16[320,1024]{1,0:T(8,128)(2,1)} %bitcast.8, bf16[1280,1024]{1,0:T(8,128)(2,1)} %wim.1, bf16[320,1024]{1,0:T(8,128)(2,1)} %wtx.1, f32[1,1]{1,0:T(1,128)} %bitcast.7.scale_ref, s32[8,128]{1,0:T(8,128)} %bitcast.9), custom_call_target="tpu_custom_call" | custom-call | tf_op jit(solution)/shard_map/pallas_call | solution.py:635
  75.2 1.3 %slice_bitcast_fusion = (f32[1024]{0:T(1024)}, f32[1024]{0:T(1024)}) fusion(f32[16,128]{1,0:T(8,128)} %shard_map.77), kind=kLoop, calls=%fused_computation | loop fusion | bytes 16384 | tf_op jit(solution)/shard_map/reshape | solution.py:682
